TPU v7x, 32 devices: a whole 2x2x4 slice. The times are simulated.
32 devices in a mesh: depth: 2 (over core), lat: 16 (over z, y, x).
Axes of the slice: x: 2, y: 2, z: 4, core: 2. Of those that a mesh axis runs over, the one named last changes fastest.
Arguments:
- fields: float32 [6, 96, 16, 512], P(None, 'lat', 'depth'), may hold values from -3 to 3
- material: int32 [96, 16, 512], P('lat', 'depth'), may hold values from 0 to 3
- source_mask: int32 [96, 16, 512], P('lat', 'depth'), may hold values 0 or 1
- eps_table: float32 [4], replicated, may hold values from 1 to 6
- kerr_table: float32 [4], replicated, may hold values from 0.3 to 3
Outputs:
- fields_out: float32 [6, 96, 16, 512], P(None, 'lat', 'depth')
- image: float32 [96, 8, 512], P('lat', None, 'depth')
Inputs may be any that keep to these rules, and one draw needn't show every extreme that they name: material indexes the tables.
All inputs are finite; a program needn't handle non-finite values. No bound on the sum of `source_mask` on one device may be relied on, other than what follows from the above.
Results may differ from a plain program's by a relative error of at most 0.0003.
Values sent between devices are 32-bit elements; how exact they have to be, the bound alone decides.
No kernel may reach another device: no remote copies, remote signals or barrier semaphores. Data moves between devices by JAX's collectives and lax.ppermute only.
A program may use at most 64 MiB of HBM per device.

v0:
```python
import math

import jax
import jax.numpy as jnp
from jax import lax
from jax.sharding import PartitionSpec as P

STEPS = 16
HALO_STEPS = 4


COURANT = 0.55
OMEGAS = (0.9, 1.3)
SOURCE_AMP = 1.0
QUARTERS = (3, 5)
HIGHEST = lax.Precision.HIGHEST


def padded_2(block, sides, width):
    for axis, dim in sides:
        count = lax.axis_size(axis)
        forward = [(i, i + 1) for i in range(count - 1)]
        backward = [(target, source) for source, target in forward]
        low = lax.ppermute(
            lax.slice_in_dim(block, block.shape[dim] - width, None, axis=dim), axis, forward
        )
        high = lax.ppermute(lax.slice_in_dim(block, 0, width, axis=dim), axis, backward)
        block = jnp.concatenate([low, block, high], axis=dim)
    return block


def from_root(block, axis, owner):
    block = jnp.where(lax.axis_index(axis) == owner, block, jnp.zeros_like(block))
    return lax.psum(block, axis)


def forward_diff(field, along):
    length = field.shape[along]
    ahead = lax.slice_in_dim(field, 1, length, axis=along)
    ahead = jnp.concatenate(
        [ahead, jnp.zeros_like(lax.slice_in_dim(field, 0, 1, axis=along))], axis=along
    )
    return ahead - field


def backward_diff(field, along):
    length = field.shape[along]
    behind = lax.slice_in_dim(field, 0, length - 1, axis=along)
    behind = jnp.concatenate(
        [jnp.zeros_like(lax.slice_in_dim(field, 0, 1, axis=along)), behind], axis=along
    )
    return field - behind


def drive(moment):
    middle = moment + 0.5
    return SOURCE_AMP * (jnp.sin(OMEGAS[0] * middle) + jnp.sin(OMEGAS[1] * middle))


def yee_step(fields, permittivity, kerr_coef, source_flag, inside, pulse):
    elec_x, elec_y, elec_z = (fields[0], fields[1], fields[2])
    magn_x, magn_y, magn_z = (fields[3], fields[4], fields[5])
    magn_x = (magn_x - COURANT * (forward_diff(elec_z, 2) - forward_diff(elec_y, 1))) * inside
    magn_y = (magn_y - COURANT * (forward_diff(elec_x, 1) - forward_diff(elec_z, 0))) * inside
    magn_z = (magn_z - COURANT * (forward_diff(elec_y, 0) - forward_diff(elec_x, 2))) * inside
    energy = elec_x * elec_x + elec_y * elec_y + elec_z * elec_z
    factor = COURANT / (permittivity + kerr_coef * energy)
    new_x = (
        elec_x
        + factor * (backward_diff(magn_z, 2) - backward_diff(magn_y, 1))
        + source_flag * pulse
    ) * inside
    new_y = (elec_y + factor * (backward_diff(magn_x, 1) - backward_diff(magn_z, 0))) * inside
    new_z = (elec_z + factor * (backward_diff(magn_y, 0) - backward_diff(magn_x, 2))) * inside
    return jnp.stack([new_x, new_y, new_z, magn_x, magn_y, magn_z])


def lookup(material, table):
    result = jnp.zeros(material.shape, jnp.float32)
    for level in range(table.shape[0]):
        result = jnp.where(material == level, table[level], result)
    return result


def accumulate(spectrum, plane, moment):
    later = moment + 1.0
    trig = jnp.stack(
        [jnp.stack([jnp.cos(omega * later), -jnp.sin(omega * later)]) for omega in OMEGAS]
    )
    return spectrum + trig[:, None, :, None, None] * plane[None, :, None, :, :]


def chirp(row_index, col_index, length):
    gap = row_index[:, None] - col_index[None, :]
    squared = gap * gap
    reals, imags = ([], [])
    for quarter in QUARTERS:
        wrapped = quarter * squared % (8 * length)
        phase = wrapped.astype(jnp.float32) * (math.pi / (4.0 * length))
        reals.append(jnp.cos(phase) / math.sqrt(length))
        imags.append(jnp.sin(phase) / math.sqrt(length))
    return (jnp.stack(reals), jnp.stack(imags))


def column_transform(real, imag, y_real, y_imag):
    v_real = jnp.einsum("fcxy,fyk->fcxk", real, y_real, precision=HIGHEST) - jnp.einsum(
        "fcxy,fyk->fcxk", imag, y_imag, precision=HIGHEST
    )
    v_imag = jnp.einsum("fcxy,fyk->fcxk", real, y_imag, precision=HIGHEST) + jnp.einsum(
        "fcxy,fyk->fcxk", imag, y_real, precision=HIGHEST
    )
    return (v_real, v_imag)


def row_transform(x_real, x_imag, v_real, v_imag):
    w_real = jnp.einsum("fix,fcxk->ifck", x_real, v_real, precision=HIGHEST) - jnp.einsum(
        "fix,fcxk->ifck", x_imag, v_imag, precision=HIGHEST
    )
    w_imag = jnp.einsum("fix,fcxk->ifck", x_real, v_imag, precision=HIGHEST) + jnp.einsum(
        "fix,fcxk->ifck", x_imag, v_real, precision=HIGHEST
    )
    return jnp.stack([w_real, w_imag], axis=3)


def local(fields, material, source_mask, eps_table, kerr_table):
    width_x = fields.shape[1]
    depth_z = fields.shape[2]
    span_y = fields.shape[3]
    lat_count = lax.axis_size("lat")
    depth_count = lax.axis_size("depth")
    total_x = width_x * lat_count
    total_z = depth_z * depth_count
    lat_pos = lax.axis_index("lat")
    depth_pos = lax.axis_index("depth")
    coefs = jnp.stack(
        [lookup(material, eps_table), lookup(material, kerr_table), source_mask.astype(jnp.float32)]
    )
    empty_spectrum = jnp.zeros((2, 2, 2, width_x, span_y), jnp.float32)
    coef_pad = padded_2(coefs, (("depth", 2), ("lat", 1)), HALO_STEPS)
    place_x = lat_pos * width_x - HALO_STEPS + jnp.arange(width_x + 2 * HALO_STEPS, dtype=jnp.int32)
    place_z = (
        depth_pos * depth_z - HALO_STEPS + jnp.arange(depth_z + 2 * HALO_STEPS, dtype=jnp.int32)
    )
    valid_x = (place_x >= 0) & (place_x < total_x)
    valid_z = (place_z >= 0) & (place_z < total_z)
    valid = valid_x[:, None] & valid_z[None, :]
    setup_inside = valid.astype(jnp.float32)[:, :, None]
    setup_permittivity = jnp.where(valid[:, :, None], coef_pad[0], 1.0)
    kerr_coef = coef_pad[1]
    source_flag = coef_pad[2]

    def one_block(block, carry):
        state, spectrum = carry
        padded = padded_2(state, (("depth", 2), ("lat", 1)), HALO_STEPS)
        for inner in range(HALO_STEPS):
            moment = (block * HALO_STEPS + inner).astype(jnp.float32)
            padded = yee_step(
                padded, setup_permittivity, kerr_coef, source_flag, setup_inside, drive(moment)
            )
            plane = padded[0:2, HALO_STEPS : HALO_STEPS + width_x, HALO_STEPS + depth_z - 1, :]
            spectrum = accumulate(spectrum, plane, moment)
        state = padded[:, HALO_STEPS : HALO_STEPS + width_x, HALO_STEPS : HALO_STEPS + depth_z]
        return (state, spectrum)

    state, spectrum = lax.fori_loop(0, STEPS // HALO_STEPS, one_block, (fields, empty_spectrum))
    spectrum = from_root(spectrum, "depth", depth_count - 1)
    col_count = span_y // depth_count
    col_index = depth_pos * col_count + jnp.arange(col_count, dtype=jnp.int32)
    y_real, y_imag = chirp(jnp.arange(span_y, dtype=jnp.int32), col_index, span_y)
    v_real, v_imag = column_transform(spectrum[:, :, 0], spectrum[:, :, 1], y_real, y_imag)
    row_local = lat_pos * width_x + jnp.arange(width_x, dtype=jnp.int32)
    row_index = jnp.arange(width_x * lax.axis_size("lat"), dtype=jnp.int32)
    x_real, x_imag = chirp(row_index, row_local, total_x)
    image = lax.psum_scatter(
        row_transform(x_real, x_imag, v_real, v_imag), "lat", scatter_dimension=0, tiled=True
    )
    return (state, image.reshape(width_x, 8, col_count))


def solution(mesh):
    placed = (
        P(None, "lat", "depth", None),
        P("lat", "depth", None),
        P("lat", "depth", None),
        P(),
        P(),
    )
    return jax.shard_map(
        local,
        mesh=mesh,
        in_specs=placed,
        out_specs=(P(None, "lat", "depth", None), P("lat", None, "depth")),
        check_vma=False,
    )
```

profile of v0, /device:TPU:0, one launch (start us, length us, event | category | flops | bytes accessed | tf_op | source)
XLA Modules:
  0.0 429.3 jit_solution(4723124953728280105)
XLA Ops:
  11.0 3.4 select_bitcast_fusion.1
  14.5 2.5 select_bitcast_fusion
  17.0 2.4 collective-permute-start.4
  20.9 1.8 collective-permute-done.5
  22.9 4.2 collective-permute-start.6
  29.0 5.1 %cosine_multiply_fusion.1 = (f32[1,512,256]{2,1,0:T(8,128)}, f32[1,512,256]{2,1,0:T(8,128)}, f32[1,512,256]{2,1,0:T(8,128)}, f32[1,512,256]{2,1,0:T(8,128)}) fusion(s32[256]{0:T(256)S(1)} %iota_add_fusion), kind=kLoop, calls=%fused_computation.100 | loop fusion | flops 4456448 | bytes 2098176 | tf_op jit(solution)/shard_map/div | solution.py:100
  34.1 10.1 %collective-permute-done.6 = f32[3,4,16,512]{3,2,1,0:T(8,128)S(1)} collective-permute-done((f32[3,4,16,512]{3,2,1,0:T(8,128)S(1)}, f32[3,4,16,512]{3,2,1,0:T(8,128)S(1)}, u32[]{:S(2)}, u32[]{:S(2)}) %collective-permute-start.6) | collective-permute-done | bytes 393248 | tf_op jit(solution)/shard_map/ppermute | solution.py:24
  44.2 1.9 collective-permute-done.7
  46.6 234.1 %while.16 = (s32[]{:T(128)}, f32[6,6,8,512]{3,2,1,0:T(8,128)S(1)}, f32[2,2,2,6,512]{4,3,2,1,0:T(8,128)S(1)}, f32[14,16,512]{2,1,0:T(8,128)S(1)}, f32[14,16,512]{...) while((s32[]{:T(128)}, f32[6,6,8,512]{3,2,1,0:T(8,128)S(1)}, ...), condition=%wide.region_1.2_spmd.clone, body=%wide.region_0.1_spmd.clone.sunk | while | flops 24691188 | bytes 132281024 | solution.py:165
  48.2 3.1 collective-permute-start.1
  55.3 5.5 %collective-permute-start.3 = (f32[6,4,16,512]{3,2,1,0:T(8,128)S(1)}, f32[6,4,16,512]{3,2,1,0:T(8,128)}, u32[]{:S(2)}, u32[]{:S(2)}) collective-permute-start(f32[6,4,16,512]{3,2,1,0:T(8,128)S(1)} %get-tuple-element.357), channel_id=1, source_target_pairs={{0,1},{1,2},{2,3},{3,4},{4,5},{5,6},{6,7},{7,8},{8,9},{9,10},{10,1... | collective-permute-start | bytes 2359304 | tf_op jit(solution)/shard_map/while/body/eval_jaxpr/ppermute | solution.py:24
  61.6 15.0 %collective-permute-done.2 = f32[6,4,16,512]{3,2,1,0:T(8,128)} collective-permute-done((f32[6,4,16,512]{3,2,1,0:T(8,128)}, f32[6,4,16,512]{3,2,1,0:T(8,128)}, u32[]{:S(2)}, u32[]{:S(2)}) %collective-permute-start.2) | collective-permute-done | bytes 786464 | tf_op jit(solution)/shard_map/while/body/eval_jaxpr/ppermute | solution.py:27
  76.6 14.7 %collective-permute-done.3 = f32[6,4,16,512]{3,2,1,0:T(8,128)} collective-permute-done((f32[6,4,16,512]{3,2,1,0:T(8,128)S(1)}, f32[6,4,16,512]{3,2,1,0:T(8,128)}, u32[]{:S(2)}, u32[]{:S(2)}) %collective-permute-start.3) | collective-permute-done | bytes 786464 | tf_op jit(solution)/shard_map/while/body/eval_jaxpr/ppermute | solution.py:24
  91.3 1.8 pad_maximum_fusion.25
  104.8 3.1 collective-permute-start.1
  111.9 6.0 %collective-permute-start.3 = (f32[6,4,16,512]{3,2,1,0:T(8,128)S(1)}, f32[6,4,16,512]{3,2,1,0:T(8,128)}, u32[]{:S(2)}, u32[]{:S(2)}) collective-permute-start(f32[6,4,16,512]{3,2,1,0:T(8,128)S(1)} %get-tuple-element.357), channel_id=1, source_target_pairs={{0,1},{1,2},{2,3},{3,4},{4,5},{5,6},{6,7},{7,8},{8,9},{9,10},{10,1... | collective-permute-start | bytes 2359304 | tf_op jit(solution)/shard_map/while/body/eval_jaxpr/ppermute | solution.py:24
  118.9 15.0 %collective-permute-done.2 = f32[6,4,16,512]{3,2,1,0:T(8,128)} collective-permute-done((f32[6,4,16,512]{3,2,1,0:T(8,128)}, f32[6,4,16,512]{3,2,1,0:T(8,128)}, u32[]{:S(2)}, u32[]{:S(2)}) %collective-permute-start.2) | collective-permute-done | bytes 786464 | tf_op jit(solution)/shard_map/while/body/eval_jaxpr/ppermute | solution.py:27
  133.8 17.1 %collective-permute-done.3 = f32[6,4,16,512]{3,2,1,0:T(8,128)} collective-permute-done((f32[6,4,16,512]{3,2,1,0:T(8,128)S(1)}, f32[6,4,16,512]{3,2,1,0:T(8,128)}, u32[]{:S(2)}, u32[]{:S(2)}) %collective-permute-start.3) | collective-permute-done | bytes 786464 | tf_op jit(solution)/shard_map/while/body/eval_jaxpr/ppermute | solution.py:24
  151.0 1.8 pad_maximum_fusion.25
  164.5 3.1 collective-permute-start.1
  171.6 6.0 %collective-permute-start.3 = (f32[6,4,16,512]{3,2,1,0:T(8,128)S(1)}, f32[6,4,16,512]{3,2,1,0:T(8,128)}, u32[]{:S(2)}, u32[]{:S(2)}) collective-permute-start(f32[6,4,16,512]{3,2,1,0:T(8,128)S(1)} %get-tuple-element.357), channel_id=1, source_target_pairs={{0,1},{1,2},{2,3},{3,4},{4,5},{5,6},{6,7},{7,8},{8,9},{9,10},{10,1... | collective-permute-start | bytes 2359304 | tf_op jit(solution)/shard_map/while/body/eval_jaxpr/ppermute | solution.py:24
  178.5 15.0 %collective-permute-done.2 = f32[6,4,16,512]{3,2,1,0:T(8,128)} collective-permute-done((f32[6,4,16,512]{3,2,1,0:T(8,128)}, f32[6,4,16,512]{3,2,1,0:T(8,128)}, u32[]{:S(2)}, u32[]{:S(2)}) %collective-permute-start.2) | collective-permute-done | bytes 786464 | tf_op jit(solution)/shard_map/while/body/eval_jaxpr/ppermute | solution.py:27
  193.5 15.5 %collective-permute-done.3 = f32[6,4,16,512]{3,2,1,0:T(8,128)} collective-permute-done((f32[6,4,16,512]{3,2,1,0:T(8,128)S(1)}, f32[6,4,16,512]{3,2,1,0:T(8,128)}, u32[]{:S(2)}, u32[]{:S(2)}) %collective-permute-start.3) | collective-permute-done | bytes 786464 | tf_op jit(solution)/shard_map/while/body/eval_jaxpr/ppermute | solution.py:24
  209.0 1.8 pad_maximum_fusion.25
  222.5 3.1 collective-permute-start.1
  229.6 6.0 %collective-permute-start.3 = (f32[6,4,16,512]{3,2,1,0:T(8,128)S(1)}, f32[6,4,16,512]{3,2,1,0:T(8,128)}, u32[]{:S(2)}, u32[]{:S(2)}) collective-permute-start(f32[6,4,16,512]{3,2,1,0:T(8,128)S(1)} %get-tuple-element.357), channel_id=1, source_target_pairs={{0,1},{1,2},{2,3},{3,4},{4,5},{5,6},{6,7},{7,8},{8,9},{9,10},{10,1... | collective-permute-start | bytes 2359304 | tf_op jit(solution)/shard_map/while/body/eval_jaxpr/ppermute | solution.py:24
  236.5 15.0 %collective-permute-done.2 = f32[6,4,16,512]{3,2,1,0:T(8,128)} collective-permute-done((f32[6,4,16,512]{3,2,1,0:T(8,128)}, f32[6,4,16,512]{3,2,1,0:T(8,128)}, u32[]{:S(2)}, u32[]{:S(2)}) %collective-permute-start.2) | collective-permute-done | bytes 786464 | tf_op jit(solution)/shard_map/while/body/eval_jaxpr/ppermute | solution.py:27
  251.5 17.1 %collective-permute-done.3 = f32[6,4,16,512]{3,2,1,0:T(8,128)} collective-permute-done((f32[6,4,16,512]{3,2,1,0:T(8,128)S(1)}, f32[6,4,16,512]{3,2,1,0:T(8,128)}, u32[]{:S(2)}, u32[]{:S(2)}) %collective-permute-start.3) | collective-permute-done | bytes 786464 | tf_op jit(solution)/shard_map/while/body/eval_jaxpr/ppermute | solution.py:24
  281.9 18.3 %all-reduce.52.cloned.1.call-done = f32[2,2,2,6,512]{4,3,1,0,2:T(8,128)} async-done(((f32[2,2,2,6,512]{4,3,1,0,2:T(8,128)}), f32[2,2,2,6,512]{4,3,1,0,2:T(8,128)}) %all-reduce.52.cloned.1.call-update) | async-done | bytes 98320 | tf_op jit(solution)/shard_map/psum | solution.py:34
  300.2 1.9 fusion.13
  302.1 1.9 convolution_add_fusion.1
  310.2 110.9 %all-reduce.54.cloned.1.call-done = f32[96,2,2,2,256]{4,3,2,1,0:T(2,128)} async-done(((f32[96,2,2,2,256]{4,3,2,1,0:T(2,128)}), f32[96,2,2,2,256]{4,3,2,1,0:T(2,128)}) %all-reduce.54.cloned.1.call-update) | async-done | bytes 786448
  (367 shorter events, 74.7 us)
Async XLA Ops:
  7.2 293.0 %all-reduce.52.cloned.1.call-start = ((), (), s32[]{:S(2)}) async-start(), calls=%async_computation | async-start | bytes 262144 | tf_op jit(solution)/shard_map/psum | solution.py:34
  17.0 3.8 collective-permute-start.4
  19.4 3.3 collective-permute-start.5
  22.9 21.3 %collective-permute-start.6 = (f32[3,4,16,512]{3,2,1,0:T(8,128)S(1)}, f32[3,4,16,512]{3,2,1,0:T(8,128)S(1)}, u32[]{:S(2)}, u32[]{:S(2)}) collective-permute-start(f32[3,4,16,512]{3,2,1,0:T(8,128)S(1)} %get-tuple-element.239), channel_id=1, source_target_pairs={{0,1},{1,2},{2,3},{3,4},{4,5},{5,6},{6,7},{7,8},{8,9},{9,10},{10,1... | collective-permute-start | bytes 1179656 | tf_op jit(solution)/shard_map/ppermute | solution.py:24
  27.1 19.0 %collective-permute-start.7 = (f32[3,4,16,512]{3,2,1,0:T(8,128)S(1)}, f32[3,4,16,512]{3,2,1,0:T(8,128)S(1)}, u32[]{:S(2)}, u32[]{:S(2)}) collective-permute-start(f32[3,4,16,512]{3,2,1,0:T(8,128)S(1)} %get-tuple-element.240), channel_id=1, source_target_pairs={{1,0},{2,1},{3,2},{4,3},{5,4},{6,5},{7,6},{8,7},{9,8},{10,9},{11,1... | collective-permute-start | bytes 1179656 | tf_op jit(solution)/shard_map/ppermute | solution.py:27
  34.1 12.4 %copy-start.1 = (f32[6,6,8,512]{3,2,1,0:T(8,128)S(1)}, f32[6,6,8,512]{3,2,1,0:T(8,128)}, u32[]{:S(2)}) copy-start(f32[6,6,8,512]{3,2,1,0:T(8,128)} %param.7) | copy-start | bytes 1769476
  46.6 235.2 %copy-start.7 = (s32[6]{0:T(128)S(1)}, s32[6]{0:T(128)}, u32[]{:S(2)}) copy-start(s32[6]{0:T(128)} %iota_add_fusion.1) | copy-start | bytes 76
  46.9 5.8 %collective-permute-start = (f32[6,6,4,512]{3,2,1,0:T(4,128)S(1)}, f32[6,6,4,512]{3,2,1,0:T(4,128)S(1)}, u32[]{:S(2)}, u32[]{:S(2)}) collective-permute-start(f32[6,6,4,512]{3,2,1,0:T(4,128)S(1)} %get-tuple-element.354), channel_id=1, source_target_pairs={{16,0},{17,1},{18,2},{19,3},{20,4},{21,5},{22,6},{23,7},{24,8},{25... | collective-permute-start | bytes 884744 | tf_op jit(solution)/shard_map/while/body/eval_jaxpr/ppermute | solution.py:27
  48.2 4.5 %collective-permute-start.1 = (f32[6,6,4,512]{3,2,1,0:T(4,128)S(1)}, f32[6,6,4,512]{3,2,1,0:T(4,128)S(1)}, u32[]{:S(2)}, u32[]{:S(2)}) collective-permute-start(f32[6,6,4,512]{3,2,1,0:T(4,128)S(1)} %get-tuple-element.355), channel_id=1, source_target_pairs={{0,16},{1,17},{2,18},{3,19},{4,20},{5,21},{6,22},{7,23},{8,24},{9,... | collective-permute-start | bytes 884744 | tf_op jit(solution)/shard_map/while/body/eval_jaxpr/ppermute | solution.py:24
  54.0 22.6 %collective-permute-start.2 = (f32[6,4,16,512]{3,2,1,0:T(8,128)}, f32[6,4,16,512]{3,2,1,0:T(8,128)}, u32[]{:S(2)}, u32[]{:S(2)}) collective-permute-start(f32[6,4,16,512]{3,2,1,0:T(8,128)} %get-tuple-element.356), channel_id=1, source_target_pairs={{1,0},{2,1},{3,2},{4,3},{5,4},{6,5},{7,6},{8,7},{9,8},{10,9},{11,1... | collective-permute-start | bytes 2359304 | tf_op jit(solution)/shard_map/while/body/eval_jaxpr/ppermute | solution.py:27
  55.3 36.0 %collective-permute-start.3 = (f32[6,4,16,512]{3,2,1,0:T(8,128)S(1)}, f32[6,4,16,512]{3,2,1,0:T(8,128)}, u32[]{:S(2)}, u32[]{:S(2)}) collective-permute-start(f32[6,4,16,512]{3,2,1,0:T(8,128)S(1)} %get-tuple-element.357), channel_id=1, source_target_pairs={{0,1},{1,2},{2,3},{3,4},{4,5},{5,6},{6,7},{7,8},{8,9},{9,10},{10,1... | collective-permute-start | bytes 2359304 | tf_op jit(solution)/shard_map/while/body/eval_jaxpr/ppermute | solution.py:24
  103.5 5.8 %collective-permute-start = (f32[6,6,4,512]{3,2,1,0:T(4,128)S(1)}, f32[6,6,4,512]{3,2,1,0:T(4,128)S(1)}, u32[]{:S(2)}, u32[]{:S(2)}) collective-permute-start(f32[6,6,4,512]{3,2,1,0:T(4,128)S(1)} %get-tuple-element.354), channel_id=1, source_target_pairs={{16,0},{17,1},{18,2},{19,3},{20,4},{21,5},{22,6},{23,7},{24,8},{25... | collective-permute-start | bytes 884744 | tf_op jit(solution)/shard_map/while/body/eval_jaxpr/ppermute | solution.py:27
  104.8 4.5 %collective-permute-start.1 = (f32[6,6,4,512]{3,2,1,0:T(4,128)S(1)}, f32[6,6,4,512]{3,2,1,0:T(4,128)S(1)}, u32[]{:S(2)}, u32[]{:S(2)}) collective-permute-start(f32[6,6,4,512]{3,2,1,0:T(4,128)S(1)} %get-tuple-element.355), channel_id=1, source_target_pairs={{0,16},{1,17},{2,18},{3,19},{4,20},{5,21},{6,22},{7,23},{8,24},{9,... | collective-permute-start | bytes 884744 | tf_op jit(solution)/shard_map/while/body/eval_jaxpr/ppermute | solution.py:24
  110.6 23.2 %collective-permute-start.2 = (f32[6,4,16,512]{3,2,1,0:T(8,128)}, f32[6,4,16,512]{3,2,1,0:T(8,128)}, u32[]{:S(2)}, u32[]{:S(2)}) collective-permute-start(f32[6,4,16,512]{3,2,1,0:T(8,128)} %get-tuple-element.356), channel_id=1, source_target_pairs={{1,0},{2,1},{3,2},{4,3},{5,4},{6,5},{7,6},{8,7},{9,8},{10,9},{11,1... | collective-permute-start | bytes 2359304 | tf_op jit(solution)/shard_map/while/body/eval_jaxpr/ppermute | solution.py:27
  111.9 39.0 %collective-permute-start.3 = (f32[6,4,16,512]{3,2,1,0:T(8,128)S(1)}, f32[6,4,16,512]{3,2,1,0:T(8,128)}, u32[]{:S(2)}, u32[]{:S(2)}) collective-permute-start(f32[6,4,16,512]{3,2,1,0:T(8,128)S(1)} %get-tuple-element.357), channel_id=1, source_target_pairs={{0,1},{1,2},{2,3},{3,4},{4,5},{5,6},{6,7},{7,8},{8,9},{9,10},{10,1... | collective-permute-start | bytes 2359304 | tf_op jit(solution)/shard_map/while/body/eval_jaxpr/ppermute | solution.py:24
  163.2 5.8 %collective-permute-start = (f32[6,6,4,512]{3,2,1,0:T(4,128)S(1)}, f32[6,6,4,512]{3,2,1,0:T(4,128)S(1)}, u32[]{:S(2)}, u32[]{:S(2)}) collective-permute-start(f32[6,6,4,512]{3,2,1,0:T(4,128)S(1)} %get-tuple-element.354), channel_id=1, source_target_pairs={{16,0},{17,1},{18,2},{19,3},{20,4},{21,5},{22,6},{23,7},{24,8},{25... | collective-permute-start | bytes 884744 | tf_op jit(solution)/shard_map/while/body/eval_jaxpr/ppermute | solution.py:27
  164.5 4.5 %collective-permute-start.1 = (f32[6,6,4,512]{3,2,1,0:T(4,128)S(1)}, f32[6,6,4,512]{3,2,1,0:T(4,128)S(1)}, u32[]{:S(2)}, u32[]{:S(2)}) collective-permute-start(f32[6,6,4,512]{3,2,1,0:T(4,128)S(1)} %get-tuple-element.355), channel_id=1, source_target_pairs={{0,16},{1,17},{2,18},{3,19},{4,20},{5,21},{6,22},{7,23},{8,24},{9,... | collective-permute-start | bytes 884744 | tf_op jit(solution)/shard_map/while/body/eval_jaxpr/ppermute | solution.py:24
  170.3 23.2 %collective-permute-start.2 = (f32[6,4,16,512]{3,2,1,0:T(8,128)}, f32[6,4,16,512]{3,2,1,0:T(8,128)}, u32[]{:S(2)}, u32[]{:S(2)}) collective-permute-start(f32[6,4,16,512]{3,2,1,0:T(8,128)} %get-tuple-element.356), channel_id=1, source_target_pairs={{1,0},{2,1},{3,2},{4,3},{5,4},{6,5},{7,6},{8,7},{9,8},{10,9},{11,1... | collective-permute-start | bytes 2359304 | tf_op jit(solution)/shard_map/while/body/eval_jaxpr/ppermute | solution.py:27
  171.6 37.4 %collective-permute-start.3 = (f32[6,4,16,512]{3,2,1,0:T(8,128)S(1)}, f32[6,4,16,512]{3,2,1,0:T(8,128)}, u32[]{:S(2)}, u32[]{:S(2)}) collective-permute-start(f32[6,4,16,512]{3,2,1,0:T(8,128)S(1)} %get-tuple-element.357), channel_id=1, source_target_pairs={{0,1},{1,2},{2,3},{3,4},{4,5},{5,6},{6,7},{7,8},{8,9},{9,10},{10,1... | collective-permute-start | bytes 2359304 | tf_op jit(solution)/shard_map/while/body/eval_jaxpr/ppermute | solution.py:24
  221.2 5.8 %collective-permute-start = (f32[6,6,4,512]{3,2,1,0:T(4,128)S(1)}, f32[6,6,4,512]{3,2,1,0:T(4,128)S(1)}, u32[]{:S(2)}, u32[]{:S(2)}) collective-permute-start(f32[6,6,4,512]{3,2,1,0:T(4,128)S(1)} %get-tuple-element.354), channel_id=1, source_target_pairs={{16,0},{17,1},{18,2},{19,3},{20,4},{21,5},{22,6},{23,7},{24,8},{25... | collective-permute-start | bytes 884744 | tf_op jit(solution)/shard_map/while/body/eval_jaxpr/ppermute | solution.py:27
  222.5 4.5 %collective-permute-start.1 = (f32[6,6,4,512]{3,2,1,0:T(4,128)S(1)}, f32[6,6,4,512]{3,2,1,0:T(4,128)S(1)}, u32[]{:S(2)}, u32[]{:S(2)}) collective-permute-start(f32[6,6,4,512]{3,2,1,0:T(4,128)S(1)} %get-tuple-element.355), channel_id=1, source_target_pairs={{0,16},{1,17},{2,18},{3,19},{4,20},{5,21},{6,22},{7,23},{8,24},{9,... | collective-permute-start | bytes 884744 | tf_op jit(solution)/shard_map/while/body/eval_jaxpr/ppermute | solution.py:24
  228.3 23.2 %collective-permute-start.2 = (f32[6,4,16,512]{3,2,1,0:T(8,128)}, f32[6,4,16,512]{3,2,1,0:T(8,128)}, u32[]{:S(2)}, u32[]{:S(2)}) collective-permute-start(f32[6,4,16,512]{3,2,1,0:T(8,128)} %get-tuple-element.356), channel_id=1, source_target_pairs={{1,0},{2,1},{3,2},{4,3},{5,4},{6,5},{7,6},{8,7},{9,8},{10,9},{11,1... | collective-permute-start | bytes 2359304 | tf_op jit(solution)/shard_map/while/body/eval_jaxpr/ppermute | solution.py:27
  229.6 39.0 %collective-permute-start.3 = (f32[6,4,16,512]{3,2,1,0:T(8,128)S(1)}, f32[6,4,16,512]{3,2,1,0:T(8,128)}, u32[]{:S(2)}, u32[]{:S(2)}) collective-permute-start(f32[6,4,16,512]{3,2,1,0:T(8,128)S(1)} %get-tuple-element.357), channel_id=1, source_target_pairs={{0,1},{1,2},{2,3},{3,4},{4,5},{5,6},{6,7},{7,8},{8,9},{9,10},{10,1... | collective-permute-start | bytes 2359304 | tf_op jit(solution)/shard_map/while/body/eval_jaxpr/ppermute | solution.py:24
  280.7 25.1 %copy-start = (f32[6,6,8,512]{3,2,1,0:T(8,128)}, f32[6,6,8,512]{3,2,1,0:T(8,128)S(1)}, u32[]{:S(2)}) copy-start(f32[6,6,8,512]{3,2,1,0:T(8,128)S(1)} %get-tuple-element.168) | copy-start | bytes 1769476
  280.7 23.7 %copy-start.4 = (f32[1,512,256]{2,1,0:T(8,128)S(1)}, f32[1,512,256]{2,1,0:T(8,128)}, u32[]{:S(2)}) copy-start(f32[1,512,256]{2,1,0:T(8,128)} %get-tuple-element.243) | copy-start | bytes 1572868
  280.7 23.7 %copy-start.5 = (f32[1,512,256]{2,1,0:T(8,128)S(1)}, f32[1,512,256]{2,1,0:T(8,128)}, u32[]{:S(2)}) copy-start(f32[1,512,256]{2,1,0:T(8,128)} %get-tuple-element.244) | copy-start | bytes 1572868
  280.8 24.4 %copy-start.2 = (f32[1,512,256]{2,1,0:T(8,128)S(1)}, f32[1,512,256]{2,1,0:T(8,128)}, u32[]{:S(2)}) copy-start(f32[1,512,256]{2,1,0:T(8,128)} %get-tuple-element.245) | copy-start | bytes 1572868
  280.8 24.4 %copy-start.3 = (f32[1,512,256]{2,1,0:T(8,128)S(1)}, f32[1,512,256]{2,1,0:T(8,128)}, u32[]{:S(2)}) copy-start(f32[1,512,256]{2,1,0:T(8,128)} %get-tuple-element.246) | copy-start | bytes 1572868
  281.5 139.6 %all-reduce.54.cloned.1.call-start = ((), (), s32[]{:S(2)}) async-start(), calls=%async_computation.1 | async-start | bytes 1572864
  300.2 4.3 %copy-start.6 = (f32[2,2,2,6,512]{4,3,1,0,2:T(8,128)S(1)}, f32[2,2,2,6,512]{4,3,1,0,2:T(8,128)}, u32[]{:S(2)}) copy-start(f32[2,2,2,6,512]{4,3,1,0,2:T(8,128)} %all-reduce.52.cloned.1.call-done) | copy-start | bytes 294916
  306.3 2.6 copy-start.8
Sparse Core Ops, SparseCore 0:
  281.6 18.5 all-reduce.51
  309.0 111.9 all-reduce.53
where the time goes:
time: 430 us; the launch traced here: 429 us
  waiting for transfers between devices  267 us (62%)
  starting transfers between devices  55.6 us (13%)
  other arithmetic  52 us (12%)
  local copies, waits for them, and re-layouts  22.5 us (5%)
  between operations  15 us (3%)
  loops' own time  9.67 us (2%)
  matrix products  7.03 us (2%)
    unnamed x3, waiting for transfers between devices  111 us
    ppermute x10, waiting for transfers between devices, padded_2(): lax.ppermute(lax.slice_in_dim(block, block.shape[dim] - width, None, axis...  74.6 us
    ppermute x10, waiting for transfers between devices, padded_2(): lax.ppermute(lax.slice_in_dim(block, 0, width, axis=dim), axis, backward)  63.6 us
    ppermute x10, starting transfers between devices, padded_2(): lax.ppermute(lax.slice_in_dim(block, block.shape[dim] - width, None, axis...  42.4 us
    psum x1, waiting for transfers between devices, from_root(): return lax.psum(block, axis)  18.3 us
    ppermute x10, starting transfers between devices, padded_2(): lax.ppermute(lax.slice_in_dim(block, 0, width, axis=dim), axis, backward)  12.9 us
    another operation x1, loops' own time, local(): lax.fori_loop(0, STEPS // HALO_STEPS, one_block, (fields, empty_spectrum))  9.67 us
    mul x12, other arithmetic, yee_step(): (elec_y + factor * (backward_diff(magn_x, 1) - backward_diff(magn_z, 0)))...  8.82 us
  transfers between devices with their start and end apart: 22, of which 13 were waited for; matrix products, arithmetic and copies ran while one was open for 2% of the time, Pallas kernels for 0%

commit v1 on v0

--- a/solution.py
+++ b/solution.py
@@ -1,8 +1,11 @@
+import functools
 import math
 
 import jax
 import jax.numpy as jnp
 from jax import lax
+from jax.experimental import pallas as pl
+from jax.experimental.pallas import tpu as pltpu
 from jax.sharding import PartitionSpec as P
 
 STEPS = 16
@@ -122,7 +125,7 @@
     return jnp.stack([w_real, w_imag], axis=3)
 
 
-def local(fields, material, source_mask, eps_table, kerr_table):
+def local_general(fields, material, source_mask, eps_table, kerr_table):
     width_x = fields.shape[1]
     depth_z = fields.shape[2]
     span_y = fields.shape[3]
@@ -177,6 +180,484 @@
     return (state, image.reshape(width_x, 8, col_count))
 
 
+GROUP = 4
+LANES = 128
+SUBS = 8
+PER_TILE = 4
+VMEM = pl.BlockSpec(memory_space=pltpu.VMEM)
+SMEM = pl.BlockSpec(memory_space=pltpu.SMEM)
+
+
+def place():
+    lat_pos = lax.axis_index("lat")
+    return lat_pos // GROUP, lat_pos % GROUP, lax.axis_index("depth")
+
+
+def call(body, out_shape, operands, in_specs=None, scratch=(), name=None):
+    return pl.pallas_call(
+        body,
+        out_shape=out_shape,
+        in_specs=in_specs or [VMEM] * len(operands),
+        out_specs=jax.tree.map(lambda _: VMEM, out_shape),
+        scratch_shapes=list(scratch),
+        compiler_params=pltpu.CompilerParams(vmem_limit_bytes=56 * 1024 * 1024),
+        name=name,
+    )(*operands)
+
+
+def f32(*shape):
+    return jax.ShapeDtypeStruct(shape, jnp.float32)
+
+
+def lane_iota(rows=SUBS):
+    return lax.broadcasted_iota(jnp.int32, (rows, LANES), 1)
+
+
+def quarters_body(pos, fields, material, mask, *pieces):
+    width_x = fields.shape[1]
+    lane = lane_iota()
+    _, member, _ = pos()
+    halo = STEPS
+
+    def row(r, _):
+        for j in range(GROUP):
+            quarter = member ^ j
+            left = jnp.maximum(quarter - 1, 0)
+            right = jnp.minimum(quarter + 1, GROUP - 1)
+            has_left = jnp.where(quarter > 0, 1.0, 0.0)
+            has_right = jnp.where(quarter < GROUP - 1, 1.0, 0.0)
+            keep = jnp.where(lane >= LANES // 2, has_left, has_right)
+
+            def read(a, block):
+                cols = pl.ds(pl.multiple_of(block * LANES, LANES), LANES)
+                if a < 6:
+                    return fields[a, r, :, cols]
+                source = material if a == 6 else mask
+                return source[r, :, cols].astype(jnp.float32)
+
+            for g in range(8 // PER_TILE):
+                packed = jnp.zeros((SUBS, LANES), jnp.float32)
+                for k in range(PER_TILE):
+                    a = g * PER_TILE + k
+                    pieces[j][r, a] = read(a, quarter)
+                    edge = jnp.where(lane >= LANES // 2, read(a, left), read(a, right)) * keep
+                    edge = pltpu.roll(edge, (2 * halo * k + halo) % LANES, 1)
+                    packed = jnp.where(lane // (2 * halo) == k, edge, packed)
+                pieces[j][r, 8 + g] = packed
+        return 0
+
+    lax.fori_loop(0, width_x, row, 0)
+
+
+def gather_rows_body(pos, p0, p1, p2, p3, own, up, down):
+    _, member, _ = pos()
+    width_x = p0.shape[0]
+    rows = GROUP * width_x
+    for j, piece in enumerate((p0, p1, p2, p3)):
+        first = (member ^ j) * width_x
+        for r in range(width_x):
+            own[first + r] = piece[r]
+    for r in range(STEPS):
+        up[r] = own[rows - STEPS + r]
+        down[r] = own[r]
+
+
+def window_tile(packed, r, a, core, lane):
+    half = LANES // 2
+    halo = STEPS
+    main = pltpu.roll(packed[r, a], (halo + half * core) % LANES, 1)
+    edge = pltpu.roll(
+        packed[r, 8 + a // PER_TILE], (half * core + LANES - 2 * halo * (a % PER_TILE)) % LANES, 1
+    )
+    below = jnp.where(core == 0, halo, 0)
+    above = jnp.where(core == 0, LANES, half + halo)
+    return jnp.where((lane < below) | (lane >= above), edge, main)
+
+
+def windows_body(pos, packed, out):
+    _, _, core = pos()
+    lane = lane_iota()
+
+    def row(r, _):
+        for a in range(8):
+            out[r, a] = window_tile(packed, r, a, 1 - core, lane)
+        return 0
+
+    lax.fori_loop(0, packed.shape[0], row, 0)
+
+
+def windows2_body(pos, low, high, out):
+    _, _, core = pos()
+    lane = lane_iota()
+
+    def row(r, _):
+        for a in range(8):
+            out[r, a] = window_tile(low, r, a, 1 - core, lane)
+            out[STEPS + r, a] = window_tile(high, r, a, 1 - core, lane)
+        return 0
+
+    lax.fori_loop(0, STEPS, row, 0)
+
+
+def trig_of(step):
+    later = step + 1.0
+    return [[math.cos(omega * later), -math.sin(omega * later)] for omega in OMEGAS]
+
+
+def steps_body(
+    pos, total_x, total_y, eps, kerr, own, low, high, theirs, theirs_halo,
+    mine_out, send_out, spec_out, field, coef, hist,
+):
+    group, member, core = pos()
+    lane = lane_iota()
+    half = LANES // 2
+    halo = STEPS
+    rows = own.shape[0]
+    span = rows + 2 * halo
+    depth = 2 * SUBS
+    levels = eps.shape[0]
+
+    def put(row, core_at, tiles):
+        subs = pl.ds(pl.multiple_of(core_at * SUBS, SUBS), SUBS)
+        for a in range(6):
+            field[row, a, subs, :] = tiles[a]
+        eps_of = jnp.zeros((SUBS, LANES), jnp.float32)
+        kerr_of = jnp.zeros((SUBS, LANES), jnp.float32)
+        for level in range(levels):
+            hit = tiles[6] == float(level)
+            eps_of = jnp.where(hit, eps[level], eps_of)
+            kerr_of = jnp.where(hit, kerr[level], kerr_of)
+        coef[row, 0, subs, :] = eps_of
+        coef[row, 1, subs, :] = kerr_of
+        coef[row, 2, subs, :] = tiles[7]
+
+    def fill(packed, at, count, other, other_at):
+        def row(r, _):
+            put(at + r, core, [window_tile(packed, r, a, core, lane) for a in range(8)])
+            put(at + r, 1 - core, [other[other_at + r, a] for a in range(8)])
+            return 0
+
+        lax.fori_loop(0, count, row, 0)
+
+    fill(own, halo, rows, theirs, 0)
+    fill(low, 0, halo, theirs_halo, 0)
+    fill(high, halo + rows, halo, theirs_halo, halo)
+
+    lane2 = lane_iota(depth)
+    sub2 = lax.broadcasted_iota(jnp.int32, (depth, LANES), 0)
+    at_y = member * LANES + core * half - halo + lane2
+    in_y = jnp.where((at_y >= 0) & (at_y < total_y), COURANT, 0.0)
+    not_top = sub2 < depth - 1
+    not_low = sub2 > 0
+
+    def next_y(f):
+        return pltpu.roll(f, LANES - 1, 1)
+
+    def prev_y(f):
+        return pltpu.roll(f, 1, 1)
+
+    def next_z(f):
+        return jnp.where(not_top, pltpu.roll(f, depth - 1, 0), 0.0)
+
+    def prev_z(f):
+        return jnp.where(not_low, pltpu.roll(f, 1, 0), 0.0)
+
+    first_x = group * rows - halo
+
+    def step(n, _):
+        middle = n.astype(jnp.float32) + 0.5
+        pulse = pulses(n)
+
+        def row(i, carry):
+            hy_behind, hz_behind = carry
+            at_x = first_x + i
+            inside = jnp.where((at_x >= 0) & (at_x < total_x), 1.0, 0.0)
+            scale = in_y * inside
+            ex, ey, ez = field[i, 0], field[i, 1], field[i, 2]
+            hx, hy, hz = field[i, 3], field[i, 4], field[i, 5]
+            ey_on, ez_on = field[i + 1, 1], field[i + 1, 2]
+            hx = hx - scale * ((next_y(ez) - ez) - (next_z(ey) - ey))
+            hy = hy - scale * ((next_z(ex) - ex) - (ez_on - ez))
+            hz = hz - scale * ((ey_on - ey) - (next_y(ex) - ex))
+            energy = ex * ex + ey * ey + ez * ez
+            factor = scale / (coef[i, 0] + coef[i, 1] * energy)
+            ex = ex + factor * ((hz - prev_y(hz)) - (hy - prev_z(hy))) + coef[i, 2] * pulse
+            ey = ey + factor * ((hx - prev_z(hx)) - (hz - hz_behind))
+            ez = ez + factor * ((hy - hy_behind) - (hx - prev_y(hx)))
+            field[i, 0], field[i, 1], field[i, 2] = ex, ey, ez
+            field[i, 3], field[i, 4], field[i, 5] = hx, hy, hz
+            hist[0, n, i] = ex[SUBS:]
+            hist[1, n, i] = ey[SUBS:]
+            return hy, hz
+
+        zero = jnp.zeros((depth, LANES), jnp.float32)
+        lax.fori_loop(n, span - 1 - n, row, (zero, zero))
+        return 0
+
+    def pulses(n):
+        value = jnp.float32(0.0)
+        for m in range(STEPS):
+            value = jnp.where(n == m, jnp.float32(drive_at(m)), value)
+        return value
+
+    lax.fori_loop(0, STEPS, step, 0)
+
+    pairs = rows // 2
+    subs_mine = pl.ds(pl.multiple_of(core * SUBS, SUBS), SUBS)
+    subs_theirs = pl.ds(pl.multiple_of((1 - core) * SUBS, SUBS), SUBS)
+
+    def pack(r, _):
+        for a in range(6):
+            for out, subs in ((mine_out, subs_mine), (send_out, subs_theirs)):
+                first = pltpu.roll(field[halo + r, a, subs, :], LANES - halo, 1)
+                second = pltpu.roll(field[halo + pairs + r, a, subs, :], half - halo, 1)
+                out[r, a] = jnp.where(lane < half, first, second)
+        return 0
+
+    lax.fori_loop(0, pairs, pack, 0)
+
+    for r0 in range(0, rows, SUBS):
+        sums = [[[None, None], [None, None]] for _ in OMEGAS]
+        for c in range(2):
+            for n in range(STEPS):
+                plane = hist[c, n, pl.ds(halo + r0, SUBS), SUBS - 1, :]
+                trig = trig_of(n)
+                for f in range(len(OMEGAS)):
+                    for part in range(2):
+                        term = trig[f][part] * plane
+                        before = sums[f][part][c]
+                        sums[f][part][c] = term if before is None else before + term
+        for f in range(len(OMEGAS)):
+            for part in range(2):
+                first = pltpu.roll(sums[f][part][0], LANES - halo, 1)
+                second = pltpu.roll(sums[f][part][1], half - halo, 1)
+                spec_out[2 * f + part, pl.ds(r0, SUBS), :] = jnp.where(lane < half, first, second)
+
+
+def drive_at(step):
+    middle = step + 0.5
+    return SOURCE_AMP * (math.sin(OMEGAS[0] * middle) + math.sin(OMEGAS[1] * middle))
+
+
+def join_body(pos, mine, theirs, *pieces):
+    _, member, core = pos()
+    lane = lane_iota()
+    half = LANES // 2
+    width_x = pieces[0].shape[0]
+    pairs = mine.shape[0]
+    for j in range(GROUP):
+        block = member ^ j
+        high = block * width_x >= pairs
+        base = block * width_x - jnp.where(high, pairs, 0)
+        for r in range(width_x):
+            for a in range(6):
+                one, two = mine[base + r, a], theirs[base + r, a]
+                first = jnp.where(core == 0, one, two)
+                second = jnp.where(core == 0, two, one)
+                low_rows = jnp.where(lane < half, first, pltpu.roll(second, half, 1))
+                high_rows = jnp.where(lane < half, pltpu.roll(first, half, 1), second)
+                pieces[j][r, a] = jnp.where(high, high_rows, low_rows)
+
+
+def unquarter_body(pos, p0, p1, p2, p3, out):
+    _, member, _ = pos()
+    for j, piece in enumerate((p0, p1, p2, p3)):
+        cols = pl.ds(pl.multiple_of((member ^ j) * LANES, LANES), LANES)
+        for r in range(piece.shape[0]):
+            for a in range(6):
+                out[a, r, :, cols] = piece[r, a]
+
+
+def chirp_parts(gap, quarter, length):
+    squared = gap * gap
+    wrapped = quarter * squared % (8 * length)
+    phase = wrapped.astype(jnp.float32) * (math.pi / (4.0 * length))
+    scale = 1.0 / math.sqrt(length)
+    return jnp.cos(phase) * scale, jnp.sin(phase) * scale
+
+
+def dot(a, b):
+    return lax.dot_general(
+        a, b, (((1,), (0,)), ((), ())), precision=HIGHEST, preferred_element_type=jnp.float32
+    )
+
+
+def row_transform_body(chirp_x, *refs):
+    pieces, outs = refs[: len(refs) - GROUP], refs[len(refs) - GROUP :]
+    for f in range(len(OMEGAS)):
+        real = jnp.concatenate([piece[2 * f] for piece in pieces], axis=0)
+        imag = jnp.concatenate([piece[2 * f + 1] for piece in pieces], axis=0)
+        both = jnp.concatenate([real, imag], axis=1)
+        by_real = dot(chirp_x[f, 0], both)
+        by_imag = dot(chirp_x[f, 1], both)
+        out_real = by_real[:, :LANES] - by_imag[:, LANES:]
+        out_imag = by_real[:, LANES:] + by_imag[:, :LANES]
+        for j in range(GROUP):
+            outs[j][2 * f] = out_real[j * SUBS : (j + 1) * SUBS]
+            outs[j][2 * f + 1] = out_imag[j * SUBS : (j + 1) * SUBS]
+
+
+def stack_body(p0, p1, p2, p3, out):
+    for j, piece in enumerate((p0, p1, p2, p3)):
+        out[j] = piece[...]
+
+
+def column_transform_body(chirp_y, mine, theirs, out):
+    half = LANES // 2
+    lane = lane_iota()
+    width_x = out.shape[0]
+    for f in range(len(OMEGAS)):
+        rows = []
+        for part in range(2):
+            for c in range(2):
+                tiles = []
+                for source in (mine, theirs):
+                    for j in range(0, GROUP, 2):
+                        one, two = source[j, 2 * f + part], source[j + 1, 2 * f + part]
+                        if c == 0:
+                            tiles.append(jnp.where(lane < half, one, pltpu.roll(two, half, 1)))
+                        else:
+                            tiles.append(jnp.where(lane < half, pltpu.roll(one, half, 1), two))
+                rows.append(jnp.concatenate(tiles, axis=1))
+        left = jnp.concatenate(rows, axis=0)
+        by_real = dot(left, chirp_y[f, 0])
+        by_imag = dot(left, chirp_y[f, 1])
+        mid = 2 * SUBS
+        out_real = by_real[:mid] - by_imag[mid:]
+        out_imag = by_imag[:mid] + by_real[mid:]
+        for c in range(2):
+            for r in range(width_x):
+                out[r, pl.ds(4 * f + 2 * c, 1), :] = out_real[c * SUBS + r : c * SUBS + r + 1]
+                out[r, pl.ds(4 * f + 2 * c + 1, 1), :] = out_imag[c * SUBS + r : c * SUBS + r + 1]
+
+
+def shift_xor(array, by):
+    count = lax.axis_size("lat")
+    return lax.ppermute(array, "lat", [(i, i ^ by) for i in range(count)])
+
+
+def swap_cores(array):
+    return lax.ppermute(array, "depth", [(0, 1), (1, 0)])
+
+
+def local_regrouped(fields, material, source_mask, eps_table, kerr_table):
+    width_x = fields.shape[1]
+    lat_count = lax.axis_size("lat")
+    groups = lat_count // GROUP
+    rows = GROUP * width_x
+    total_x = width_x * lat_count
+    span_y = fields.shape[3]
+    group, member, core = place()
+
+    pieces = call(
+        functools.partial(quarters_body, place),
+        [f32(width_x, 10, SUBS, LANES)] * GROUP,
+        (fields, material, source_mask),
+        name="quarters",
+    )
+    pieces = [pieces[0]] + [shift_xor(pieces[j], j) for j in range(1, GROUP)]
+
+    j_of = jnp.arange(GROUP * SUBS, dtype=jnp.int32) // SUBS
+    r_of = jnp.arange(GROUP * SUBS, dtype=jnp.int32) % SUBS
+    x_out = group * rows + (member ^ j_of) * width_x + r_of
+    k_of = jnp.arange(total_x, dtype=jnp.int32)
+    x_in = (group ^ (k_of // rows)) * rows + k_of % rows
+    x_gap = x_out[:, None] - x_in[None, :]
+    chirp_x = jnp.stack([jnp.stack(chirp_parts(x_gap, q, total_x)) for q in QUARTERS])
+    half = LANES // 2
+    col_count = span_y // 2
+    k_of = jnp.arange(span_y, dtype=jnp.int32)
+    source = k_of // (GROUP * half)
+    y_in = (
+        LANES * (member ^ (k_of // half % GROUP)) + half * (core ^ source) + k_of % half
+    )
+    y_out = core * col_count + jnp.arange(col_count, dtype=jnp.int32)
+    y_gap = y_in[:, None] - y_out[None, :]
+    chirp_y = jnp.stack([jnp.stack(chirp_parts(y_gap, q, span_y)) for q in QUARTERS])
+
+    own, up, down = call(
+        functools.partial(gather_rows_body, place),
+        [f32(rows, 10, SUBS, LANES), f32(STEPS, 10, SUBS, LANES), f32(STEPS, 10, SUBS, LANES)],
+        pieces,
+        name="gather_rows",
+    )
+    upward = [(i, i + GROUP) for i in range(lat_count - GROUP)]
+    low = lax.ppermute(up, "lat", upward)
+    high = lax.ppermute(down, "lat", [(b, a) for a, b in upward])
+    theirs = swap_cores(
+        call(functools.partial(windows_body, place), f32(rows, 8, SUBS, LANES), (own,), name="win")
+    )
+    theirs_halo = swap_cores(
+        call(
+            functools.partial(windows2_body, place),
+            f32(2 * STEPS, 8, SUBS, LANES),
+            (low, high),
+            name="win_halo",
+        )
+    )
+    span = rows + 2 * STEPS
+    mine, send, spec = call(
+        functools.partial(steps_body, place, total_x, span_y),
+        [
+            f32(rows // 2, 6, SUBS, LANES),
+            f32(rows // 2, 6, SUBS, LANES),
+            f32(4, rows, LANES),
+        ],
+        (eps_table, kerr_table, own, low, high, theirs, theirs_halo),
+        in_specs=[SMEM, SMEM] + [VMEM] * 5,
+        scratch=[
+            pltpu.VMEM((span, 6, 2 * SUBS, LANES), jnp.float32),
+            pltpu.VMEM((span, 3, 2 * SUBS, LANES), jnp.float32),
+            pltpu.VMEM((2, STEPS, span, SUBS, LANES), jnp.float32),
+        ],
+        name="steps",
+    )
+    specs = [spec] + [shift_xor(spec, GROUP * k) for k in range(1, groups)]
+    joined = call(
+        functools.partial(join_body, place),
+        [f32(width_x, 6, SUBS, LANES)] * GROUP,
+        (mine, swap_cores(send)),
+        name="join",
+    )
+    joined = [joined[0]] + [shift_xor(joined[j], j) for j in range(1, GROUP)]
+    turned = call(row_transform_body, [f32(4, SUBS, LANES)] * GROUP, [chirp_x] + specs, name="rowt")
+    turned = [turned[0]] + [shift_xor(turned[j], j) for j in range(1, GROUP)]
+    stacked = call(stack_body, f32(GROUP, 4, SUBS, LANES), turned, name="stack")
+    image = call(
+        column_transform_body,
+        f32(width_x, 8, col_count),
+        (chirp_y, stacked, swap_cores(stacked)),
+        name="colt",
+    )
+    state = call(
+        functools.partial(unquarter_body, place),
+        f32(6, width_x, SUBS, span_y),
+        joined,
+        name="unquarter",
+    )
+    return state, image
+
+
+def can_regroup(fields, eps_table):
+    lat_count = lax.axis_size("lat")
+    groups = lat_count // GROUP
+    return (
+        lax.axis_size("depth") == 2
+        and lat_count % GROUP == 0
+        and groups & (groups - 1) == 0
+        and fields.shape[1] <= SUBS
+        and (GROUP * fields.shape[1]) % SUBS == 0
+        and GROUP * fields.shape[1] >= STEPS
+        and fields.shape[2] == SUBS
+        and fields.shape[3] == GROUP * LANES
+    )
+
+
+def local(fields, material, source_mask, eps_table, kerr_table):
+    run = local_regrouped if can_regroup(fields, eps_table) else local_general
+    return run(fields, material, source_mask, eps_table, kerr_table)
+
+
 def solution(mesh):
     placed = (
         P(None, "lat", "depth", None),

time: 430 us -> 202 us (0.47)
  waiting for transfers between devices: 267 us -> 35.8 us
  Pallas kernels: 0 us -> 130 us
  other arithmetic: 52 us -> 6.83 us
  starting transfers between devices: 55.6 us -> 21.2 us
  local copies, waits for them, and re-layouts: 22.5 us -> 7.39 us
  between operations: 15 us -> 0.75 us
  loops' own time: 9.67 us -> 0 us
  matrix products: 7.03 us -> 0 us
    pallas_call x0 -> x10, Pallas kernels: none -> 130 us  [call(): pl.pallas_call(body, out_shape=out_shape, in_specs=in_specs or [VMEM] * l...]
    unnamed x3 -> x0, waiting for transfers between devices: 111 us -> none
    ppermute x20 -> x18, waiting for transfers between devices: 138 us -> 35.8 us  [the longest x12 19.9 us: shift_xor(): return lax.ppermute(array, 'lat', [(i, i ^ by) for i in range(count)])]
    ppermute x20 -> x18, starting transfers between devices: 55.3 us -> 21.2 us  [the longest x12 15.9 us: shift_xor(): return lax.ppermute(array, 'lat', [(i, i ^ by) for i in range(count)])]
    mul x44 -> x2, other arithmetic: 23.4 us -> 4.48 us  [chirp_parts(): return (jnp.cos(phase) * scale, jnp.sin(phase) * scale)]
    psum x1 -> x0, waiting for transfers between devices: 18.3 us -> none  [from_root(): return lax.psum(block, axis)]
    slice x156 -> x0, local copies, waits for them, and re-layouts: 17.8 us -> none  [the longest x92 8.37 us: forward_diff(): ahead = lax.slice_in_dim(field, 1, length, axis=along)]
    another operation x1 -> x0, loops' own time: 9.67 us -> none  [local(): lax.fori_loop(0, STEPS // HALO_STEPS, one_block, (fields, empty_spectrum))]
  transfers between devices with their start and end apart: 22 -> 18, of which waited for: 13 -> 9; matrix products, arithmetic and copies ran while one was open for 2% -> 3% of each run, Pallas kernels for 0% -> 6%
where the time goes in v1:
time: 202 us
  Pallas kernels  130 us (64%)
  waiting for transfers between devices  35.8 us (18%)
  starting transfers between devices  21.2 us (10%)
  local copies, waits for them, and re-layouts  7.39 us (4%)
  other arithmetic  6.83 us (3%)
    pallas_call x10, Pallas kernels, call(): pl.pallas_call(body, out_shape=out_shape, in_specs=in_specs or [VMEM] * l...  130 us
    ppermute x12, waiting for transfers between devices, shift_xor(): return lax.ppermute(array, 'lat', [(i, i ^ by) for i in range(count)])  19.9 us
    ppermute x12, starting transfers between devices, shift_xor(): return lax.ppermute(array, 'lat', [(i, i ^ by) for i in range(count)])  15.9 us
    ppermute x1, waiting for transfers between devices, local_regrouped(): low = lax.ppermute(up, 'lat', upward)  11.8 us
    unnamed x36, local copies, waits for them, and re-layouts  7.39 us
    mul x2, other arithmetic, chirp_parts(): return (jnp.cos(phase) * scale, jnp.sin(phase) * scale)  4.48 us
    ppermute x1, waiting for transfers between devices, local_regrouped(): high = lax.ppermute(down, 'lat', [(b, a) for a, b in upward])  4.05 us
  transfers between devices with their start and end apart: 18, of which 9 were waited for; matrix products, arithmetic and copies ran while one was open for 3% of the time, Pallas kernels for 6%

profile of v1, /device:TPU:0, one launch (start us, length us, event | category | flops | bytes accessed | tf_op | source)
XLA Modules:
  0.0 202.0 jit_solution(15131965677351696050)
XLA Ops:
  0.6 2.8 %quarters.1 = (f32[6,10,8,128]{3,2,1,0:T(8,128)}, f32[6,10,8,128]{3,2,1,0:T(8,128)}, f32[6,10,8,128]{3,2,1,0:T(8,128)}, f32[6,10,8,128]{3,2,1,0:T(8,128)}) custom-call(f32[6,6,8,512]{3,2,1,0:T(8,128)} %fields.1, s32[6,8,512]{2,1,0:T(8,128)} %material.1, s32[6,8,512]{2,1,0:T(8,128)} %mask.1), custom_call_target="tpu_custom_call" | custom-call | tf_op jit(solution)/shard_map/quarters/pallas_call | solution.py:197
  3.4 3.0 %collective-permute-start = (f32[6,10,8,128]{3,2,1,0:T(8,128)}, f32[6,10,8,128]{3,2,1,0:T(8,128)S(1)}, u32[]{:S(2)}, u32[]{:S(2)}) collective-permute-start(f32[6,10,8,128]{3,2,1,0:T(8,128)} %get-tuple-element.21), channel_id=1, source_target_pairs={{0,1},{1,0},{2,3},{3,2},{4,5},{5,4},{6,7},{7,6},{8,9},{9,8},{10,11... | collective-permute-start | bytes 737288 | tf_op jit(solution)/shard_map/ppermute | solution.py:536
  6.4 1.5 collective-permute-start.1
  7.9 5.5 %collective-permute-done.p1 = f32[6,10,8,128]{3,2,1,0:T(8,128)S(1)} collective-permute-done((f32[6,10,8,128]{3,2,1,0:T(8,128)}, f32[6,10,8,128]{3,2,1,0:T(8,128)S(1)}, u32[]{:S(2)}, u32[]{:S(2)}) %collective-permute-start) | collective-permute-done | bytes 245792 | tf_op jit(solution)/shard_map/ppermute | solution.py:536
  13.4 5.9 %collective-permute-done.1.p2 = f32[6,10,8,128]{3,2,1,0:T(8,128)S(1)} collective-permute-done((f32[6,10,8,128]{3,2,1,0:T(8,128)}, f32[6,10,8,128]{3,2,1,0:T(8,128)S(1)}, u32[]{:S(2)}, u32[]{:S(2)}) %collective-permute-start.1) | collective-permute-done | bytes 245792 | tf_op jit(solution)/shard_map/ppermute | solution.py:536
  20.1 2.8 %gather_rows.1 = (f32[24,10,8,128]{3,2,1,0:T(8,128)}, f32[16,10,8,128]{3,2,1,0:T(8,128)}, f32[16,10,8,128]{3,2,1,0:T(8,128)}) custom-call(f32[6,10,8,128]{3,2,1,0:T(8,128)} %get-tuple-element.20.p0, f32[6,10,8,128]{3,2,1,0:T(8,128)} %copy-done.5, f32[6,10,8,128]{3,2,1,0:T(8,128)} %copy-done.6, f32[6,10,8,128]{3,2,1,0:T(8,128)} %copy-done.7), custom_call_target="tpu_custom_call" | custom-call | tf_op jit(solution)/shard_map/gather_rows/pallas_call | solution.py:197
  22.8 3.5 %collective-permute-start.3 = (f32[16,10,8,128]{3,2,1,0:T(8,128)}, f32[16,10,8,128]{3,2,1,0:T(8,128)S(1)}, u32[]{:S(2)}, u32[]{:S(2)}) collective-permute-start(f32[16,10,8,128]{3,2,1,0:T(8,128)} %get-tuple-element.25), channel_id=1, source_target_pairs={{0,4},{1,5},{2,6},{3,7},{4,8},{5,9},{6,10},{7,11},{8,12},{9,13},{1... | collective-permute-start | bytes 1966088 | tf_op jit(solution)/shard_map/ppermute | solution.py:585
  26.3 1.3 collective-permute-start.4
  27.6 11.8 %collective-permute-done.3.low = f32[16,10,8,128]{3,2,1,0:T(8,128)S(1)} collective-permute-done((f32[16,10,8,128]{3,2,1,0:T(8,128)}, f32[16,10,8,128]{3,2,1,0:T(8,128)S(1)}, u32[]{:S(2)}, u32[]{:S(2)}) %collective-permute-start.3) | collective-permute-done | bytes 655392 | tf_op jit(solution)/shard_map/ppermute | solution.py:585
  39.4 4.0 %collective-permute-done.4.high = f32[16,10,8,128]{3,2,1,0:T(8,128)S(1)} collective-permute-done((f32[16,10,8,128]{3,2,1,0:T(8,128)}, f32[16,10,8,128]{3,2,1,0:T(8,128)S(1)}, u32[]{:S(2)}, u32[]{:S(2)}) %collective-permute-start.4) | collective-permute-done | bytes 655392 | tf_op jit(solution)/shard_map/ppermute | solution.py:586
  44.3 3.9 %win_halo.1 = f32[32,8,8,128]{3,2,1,0:T(8,128)} custom-call(f32[16,10,8,128]{3,2,1,0:T(8,128)} %copy-done, f32[16,10,8,128]{3,2,1,0:T(8,128)} %copy-done.1), custom_call_target="tpu_custom_call" | custom-call | tf_op jit(solution)/shard_map/win_halo/pallas_call | solution.py:197
  48.2 4.2 %win.1 = f32[24,8,8,128]{3,2,1,0:T(8,128)} custom-call(f32[24,10,8,128]{3,2,1,0:T(8,128)} %get-tuple-element.24.packed.own), custom_call_target="tpu_custom_call" | custom-call | tf_op jit(solution)/shard_map/win/pallas_call | solution.py:197
  53.1 4.3 %cosine_multiply_fusion.1 = (f32[1,512,256]{2,1,0:T(8,128)S(1)}, f32[1,512,256]{2,1,0:T(8,128)S(1)}, f32[1,512,256]{2,1,0:T(8,128)S(1)}, f32[1,512,256]{2,1,0:T(8,128)S(1)}) fusion(s32[256]{0:T(256)S(1)} %iota_add_fusion, s32[512]{0:T(512)S(1)} %fusion.24), kind=kLoop, calls=%fused_computation.18 | loop fusion | flops 4456448 | bytes 2100224 | tf_op jit(solution)/shard_map/mul | solution.py:476
  58.3 1.0 copy-done.2
  59.3 105.7 %steps.1 = (f32[12,6,8,128]{3,2,1,0:T(8,128)}, f32[12,6,8,128]{3,2,1,0:T(8,128)}, f32[4,24,128]{2,1,0:T(8,128)}) custom-call(f32[4]{0:T(128)} %eps.1, f32[4]{0:T(128)} %kerr.1, f32[24,10,8,128]{3,2,1,0:T(8,128)} %get-tuple-element.24.packed.own, f32[16,10,8,128]{3,2,1,0:T(8,128)} %copy-done, f32[16,10,8,128]{3,2,1,0:T(8,128)} %copy-done.1, ...), custom_call_target="tpu_custom_call" | custom-call | tf_op jit(solution)/shard_map/steps/pallas_call | solution.py:197
  165.0 1.6 collective-permute-start.11
  166.6 1.1 collective-permute-start.12
  167.7 1.8 collective-permute-start.13
  170.1 3.9 %collective-permute-done.12.refs_2_ = f32[4,24,128]{2,1,0:T(8,128)S(1)} collective-permute-done((f32[4,24,128]{2,1,0:T(8,128)}, f32[4,24,128]{2,1,0:T(8,128)S(1)}, u32[]{:S(2)}, u32[]{:S(2)}) %collective-permute-start.12) | collective-permute-done | bytes 49184 | tf_op jit(solution)/shard_map/ppermute | solution.py:536
  175.3 1.8 rowt.1
  177.1 1.4 collective-permute-start.14
  179.1 1.5 collective-permute-start.16
  181.0 1.4 collective-permute-done.15.p2
  182.5 1.5 collective-permute-done.16.p3
  184.5 1.4 stack.49.mine
  186.7 2.1 %join.1 = (f32[6,6,8,128]{3,2,1,0:T(8,128)}, f32[6,6,8,128]{3,2,1,0:T(8,128)}, f32[6,6,8,128]{3,2,1,0:T(8,128)}, f32[6,6,8,128]{3,2,1,0:T(8,128)}) custom-call(f32[12,6,8,128]{3,2,1,0:T(8,128)} %get-tuple-element.27.mine, f32[12,6,8,128]{3,2,1,0:T(8,128)} %copy-done.4), custom_call_target="tpu_custom_call" | custom-call | tf_op jit(solution)/shard_map/join/pallas_call | solution.py:197
  188.7 1.5 collective-permute-start.10
  190.2 1.4 collective-permute-start.8
  192.2 1.5 pad_maximum_fusion.chirp_y
  194.4 3.5 %colt.1 = f32[6,8,256]{2,1,0:T(8,128)} custom-call(f32[2,2,512,256]{3,2,1,0:T(8,128)} %pad_maximum_fusion.chirp_y, f32[4,4,8,128]{3,2,1,0:T(8,128)} %stack.49.mine, f32[4,4,8,128]{3,2,1,0:T(8,128)} %copy-done.11), custom_call_target="tpu_custom_call" | custom-call | tf_op jit(solution)/shard_map/colt/pallas_call | solution.py:197
  197.9 1.5 collective-permute-done.8.p1
  200.0 2.0 unquarter.1
  (60 shorter events, 9.4 us)
Async XLA Ops:
  3.4 10.0 %collective-permute-start = (f32[6,10,8,128]{3,2,1,0:T(8,128)}, f32[6,10,8,128]{3,2,1,0:T(8,128)S(1)}, u32[]{:S(2)}, u32[]{:S(2)}) collective-permute-start(f32[6,10,8,128]{3,2,1,0:T(8,128)} %get-tuple-element.21), channel_id=1, source_target_pairs={{0,1},{1,0},{2,3},{3,2},{4,5},{5,4},{6,7},{7,6},{8,9},{9,8},{10,11... | collective-permute-start | bytes 737288 | tf_op jit(solution)/shard_map/ppermute | solution.py:536
  6.4 12.9 %collective-permute-start.1 = (f32[6,10,8,128]{3,2,1,0:T(8,128)}, f32[6,10,8,128]{3,2,1,0:T(8,128)S(1)}, u32[]{:S(2)}, u32[]{:S(2)}) collective-permute-start(f32[6,10,8,128]{3,2,1,0:T(8,128)} %get-tuple-element.22), channel_id=1, source_target_pairs={{0,2},{1,3},{2,0},{3,1},{4,6},{5,7},{6,4},{7,5},{8,10},{9,11},{10,... | collective-permute-start | bytes 737288 | tf_op jit(solution)/shard_map/ppermute | solution.py:536
  7.9 11.4 %collective-permute-start.2 = (f32[6,10,8,128]{3,2,1,0:T(8,128)}, f32[6,10,8,128]{3,2,1,0:T(8,128)S(1)}, u32[]{:S(2)}, u32[]{:S(2)}) collective-permute-start(f32[6,10,8,128]{3,2,1,0:T(8,128)} %get-tuple-element.23), channel_id=1, source_target_pairs={{0,3},{1,2},{2,1},{3,0},{4,7},{5,6},{6,5},{7,4},{8,11},{9,10},{10,... | collective-permute-start | bytes 737288 | tf_op jit(solution)/shard_map/ppermute | solution.py:536
  13.4 5.9 %copy-start.5 = (f32[6,10,8,128]{3,2,1,0:T(8,128)}, f32[6,10,8,128]{3,2,1,0:T(8,128)S(1)}, u32[]{:S(2)}) copy-start(f32[6,10,8,128]{3,2,1,0:T(8,128)S(1)} %collective-permute-done.p1) | copy-start | bytes 737284
  19.3 0.7 copy-start.6
  19.3 0.8 copy-start.7
  22.8 16.6 %collective-permute-start.3 = (f32[16,10,8,128]{3,2,1,0:T(8,128)}, f32[16,10,8,128]{3,2,1,0:T(8,128)S(1)}, u32[]{:S(2)}, u32[]{:S(2)}) collective-permute-start(f32[16,10,8,128]{3,2,1,0:T(8,128)} %get-tuple-element.25), channel_id=1, source_target_pairs={{0,4},{1,5},{2,6},{3,7},{4,8},{5,9},{6,10},{7,11},{8,12},{9,13},{1... | collective-permute-start | bytes 1966088 | tf_op jit(solution)/shard_map/ppermute | solution.py:585
  26.3 17.1 %collective-permute-start.4 = (f32[16,10,8,128]{3,2,1,0:T(8,128)}, f32[16,10,8,128]{3,2,1,0:T(8,128)S(1)}, u32[]{:S(2)}, u32[]{:S(2)}) collective-permute-start(f32[16,10,8,128]{3,2,1,0:T(8,128)} %get-tuple-element.26), channel_id=1, source_target_pairs={{4,0},{5,1},{6,2},{7,3},{8,4},{9,5},{10,6},{11,7},{12,8},{13,9},{1... | collective-permute-start | bytes 1966088 | tf_op jit(solution)/shard_map/ppermute | solution.py:586
  39.4 4.1 %copy-start = (f32[16,10,8,128]{3,2,1,0:T(8,128)}, f32[16,10,8,128]{3,2,1,0:T(8,128)S(1)}, u32[]{:S(2)}) copy-start(f32[16,10,8,128]{3,2,1,0:T(8,128)S(1)} %collective-permute-done.3.low) | copy-start | bytes 1966084
  43.5 0.9 copy-start.1
  48.2 9.2 %collective-permute-start.6 = (f32[32,8,8,128]{3,2,1,0:T(8,128)}, f32[32,8,8,128]{3,2,1,0:T(8,128)S(1)}, u32[]{:S(2)}, u32[]{:S(2)}) collective-permute-start(f32[32,8,8,128]{3,2,1,0:T(8,128)} %win_halo.1), channel_id=1, source_target_pairs={{0,16},{16,0},{1,17},{17,1},{2,18},{18,2},{3,19},{19,3},{4,20},{20... | collective-permute-start | bytes 3145736 | tf_op jit(solution)/shard_map/ppermute | solution.py:540
  52.4 5.0 %collective-permute-start.5 = (f32[24,8,8,128]{3,2,1,0:T(8,128)}, f32[24,8,8,128]{3,2,1,0:T(8,128)S(1)}, u32[]{:S(2)}, u32[]{:S(2)}) collective-permute-start(f32[24,8,8,128]{3,2,1,0:T(8,128)} %win.1), channel_id=1, source_target_pairs={{0,16},{16,0},{1,17},{17,1},{2,18},{18,2},{3,19},{19,3},{4,20},{20... | collective-permute-start | bytes 2359304 | tf_op jit(solution)/shard_map/ppermute | solution.py:540
  57.4 0.9 copy-start.3
  58.3 1.0 copy-start.2
  165.0 20.9 %collective-permute-start.7 = (f32[12,6,8,128]{3,2,1,0:T(8,128)}, f32[12,6,8,128]{3,2,1,0:T(8,128)S(1)}, u32[]{:S(2)}, u32[]{:S(2)}) collective-permute-start(f32[12,6,8,128]{3,2,1,0:T(8,128)} %get-tuple-element.28), channel_id=1, source_target_pairs={{0,16},{16,0},{1,17},{17,1},{2,18},{18,2},{3,19},{19,3},{4,20},{20... | collective-permute-start | bytes 884744 | tf_op jit(solution)/shard_map/ppermute | solution.py:540
  165.0 5.1 %collective-permute-start.11 = (f32[4,24,128]{2,1,0:T(8,128)}, f32[4,24,128]{2,1,0:T(8,128)S(1)}, u32[]{:S(2)}, u32[]{:S(2)}) collective-permute-start(f32[4,24,128]{2,1,0:T(8,128)} %get-tuple-element.33.refs_0_), channel_id=1, source_target_pairs={{0,4},{1,5},{2,6},{3,7},{4,0},{5,1},{6,2},{7,3},{8,12},{9,13},{10,... | collective-permute-start | bytes 147464 | tf_op jit(solution)/shard_map/ppermute | solution.py:536
  166.6 7.4 %collective-permute-start.12 = (f32[4,24,128]{2,1,0:T(8,128)}, f32[4,24,128]{2,1,0:T(8,128)S(1)}, u32[]{:S(2)}, u32[]{:S(2)}) collective-permute-start(f32[4,24,128]{2,1,0:T(8,128)} %get-tuple-element.33.refs_0_), channel_id=1, source_target_pairs={{0,8},{1,9},{2,10},{3,11},{4,12},{5,13},{6,14},{7,15},{8,0},{9,1},... | collective-permute-start | bytes 147464 | tf_op jit(solution)/shard_map/ppermute | solution.py:536
  167.7 6.3 %collective-permute-start.13 = (f32[4,24,128]{2,1,0:T(8,128)}, f32[4,24,128]{2,1,0:T(8,128)S(1)}, u32[]{:S(2)}, u32[]{:S(2)}) collective-permute-start(f32[4,24,128]{2,1,0:T(8,128)} %get-tuple-element.33.refs_0_), channel_id=1, source_target_pairs={{0,12},{1,13},{2,14},{3,15},{4,8},{5,9},{6,10},{7,11},{8,4},{9,5},... | collective-permute-start | bytes 147464 | tf_op jit(solution)/shard_map/ppermute | solution.py:536
  170.1 3.9 %copy-start.12 = (f32[4,24,128]{2,1,0:T(8,128)}, f32[4,24,128]{2,1,0:T(8,128)S(1)}, u32[]{:S(2)}) copy-start(f32[4,24,128]{2,1,0:T(8,128)S(1)} %collective-permute-done.11.refs_1_) | copy-start | bytes 147460
  177.1 3.9 %collective-permute-start.14 = (f32[4,8,128]{2,1,0:T(8,128)}, f32[4,8,128]{2,1,0:T(8,128)S(1)}, u32[]{:S(2)}, u32[]{:S(2)}) collective-permute-start(f32[4,8,128]{2,1,0:T(8,128)} %get-tuple-element.35), channel_id=1, source_target_pairs={{0,1},{1,0},{2,3},{3,2},{4,5},{5,4},{6,7},{7,6},{8,9},{9,8},{10,11... | collective-permute-start | bytes 49160 | tf_op jit(solution)/shard_map/ppermute | solution.py:536
  178.5 3.9 %collective-permute-start.15 = (f32[4,8,128]{2,1,0:T(8,128)}, f32[4,8,128]{2,1,0:T(8,128)S(1)}, u32[]{:S(2)}, u32[]{:S(2)}) collective-permute-start(f32[4,8,128]{2,1,0:T(8,128)} %get-tuple-element.36), channel_id=1, source_target_pairs={{0,2},{1,3},{2,0},{3,1},{4,6},{5,7},{6,4},{7,5},{8,10},{9,11},{10,... | collective-permute-start | bytes 49160 | tf_op jit(solution)/shard_map/ppermute | solution.py:536
  179.1 4.8 %collective-permute-start.16 = (f32[4,8,128]{2,1,0:T(8,128)}, f32[4,8,128]{2,1,0:T(8,128)S(1)}, u32[]{:S(2)}, u32[]{:S(2)}) collective-permute-start(f32[4,8,128]{2,1,0:T(8,128)} %get-tuple-element.37), channel_id=1, source_target_pairs={{0,3},{1,2},{2,1},{3,0},{4,7},{5,6},{6,5},{7,4},{8,11},{9,10},{10,... | collective-permute-start | bytes 49160 | tf_op jit(solution)/shard_map/ppermute | solution.py:536
  181.0 2.9 %copy-start.15 = (f32[4,8,128]{2,1,0:T(8,128)}, f32[4,8,128]{2,1,0:T(8,128)S(1)}, u32[]{:S(2)}) copy-start(f32[4,8,128]{2,1,0:T(8,128)S(1)} %collective-permute-done.14.p1) | copy-start | bytes 49156
  182.5 1.5 copy-start.16
  185.9 7.8 %collective-permute-start.17 = (f32[4,4,8,128]{3,2,1,0:T(8,128)}, f32[4,4,8,128]{3,2,1,0:T(8,128)S(1)}, u32[]{:S(2)}, u32[]{:S(2)}) collective-permute-start(f32[4,4,8,128]{3,2,1,0:T(8,128)} %stack.49.mine), channel_id=1, source_target_pairs={{0,16},{16,0},{1,17},{17,1},{2,18},{18,2},{3,19},{19,3},{4,20},{20... | collective-permute-start | bytes 196616 | tf_op jit(solution)/shard_map/ppermute | solution.py:540
  185.9 0.7 copy-start.4
  188.7 9.1 %collective-permute-start.10 = (f32[6,6,8,128]{3,2,1,0:T(8,128)}, f32[6,6,8,128]{3,2,1,0:T(8,128)S(1)}, u32[]{:S(2)}, u32[]{:S(2)}) collective-permute-start(f32[6,6,8,128]{3,2,1,0:T(8,128)} %get-tuple-element.32), channel_id=1, source_target_pairs={{0,3},{1,2},{2,1},{3,0},{4,7},{5,6},{6,5},{7,4},{8,11},{9,10},{10,... | collective-permute-start | bytes 442376 | tf_op jit(solution)/shard_map/ppermute | solution.py:536
  190.2 9.1 %collective-permute-start.8 = (f32[6,6,8,128]{3,2,1,0:T(8,128)}, f32[6,6,8,128]{3,2,1,0:T(8,128)S(1)}, u32[]{:S(2)}, u32[]{:S(2)}) collective-permute-start(f32[6,6,8,128]{3,2,1,0:T(8,128)} %get-tuple-element.30), channel_id=1, source_target_pairs={{0,1},{1,0},{2,3},{3,2},{4,5},{5,4},{6,7},{7,6},{8,9},{9,8},{10,11... | collective-permute-start | bytes 442376 | tf_op jit(solution)/shard_map/ppermute | solution.py:536
  191.7 7.7 %collective-permute-start.9 = (f32[6,6,8,128]{3,2,1,0:T(8,128)}, f32[6,6,8,128]{3,2,1,0:T(8,128)S(1)}, u32[]{:S(2)}, u32[]{:S(2)}) collective-permute-start(f32[6,6,8,128]{3,2,1,0:T(8,128)} %get-tuple-element.31), channel_id=1, source_target_pairs={{0,2},{1,3},{2,0},{3,1},{4,6},{5,7},{6,4},{7,5},{8,10},{9,11},{10,... | collective-permute-start | bytes 442376 | tf_op jit(solution)/shard_map/ppermute | solution.py:536
  197.9 1.5 copy-start.8
  199.3 0.7 copy-start.9
  199.3 0.7 copy-start.10
  (4 other events, 2.5 us)

commit v2 on v1

--- a/solution.py
+++ b/solution.py
@@ -184,6 +184,7 @@
 LANES = 128
 SUBS = 8
 PER_TILE = 4
+UNROLL = 8
 VMEM = pl.BlockSpec(memory_space=pltpu.VMEM)
 SMEM = pl.BlockSpec(memory_space=pltpu.SMEM)
 
@@ -193,12 +194,18 @@
     return lat_pos // GROUP, lat_pos % GROUP, lax.axis_index("depth")
 
 
-def call(body, out_shape, operands, in_specs=None, scratch=(), name=None):
+def call(body, out_shape, operands, in_specs=None, scratch=(), name=None, near=True):
+    if near:
+        specs = in_specs or [VMEM] * len(operands)
+        operands = [
+            pltpu.with_memory_space_constraint(operand, pltpu.VMEM) if spec is VMEM else operand
+            for operand, spec in zip(operands, specs)
+        ]
     return pl.pallas_call(
         body,
         out_shape=out_shape,
         in_specs=in_specs or [VMEM] * len(operands),
-        out_specs=jax.tree.map(lambda _: VMEM, out_shape),
+        out_specs=[VMEM] * len(out_shape) if isinstance(out_shape, list) else VMEM,
         scratch_shapes=list(scratch),
         compiler_params=pltpu.CompilerParams(vmem_limit_bytes=56 * 1024 * 1024),
         name=name,
@@ -206,6 +213,10 @@
 
 
 def f32(*shape):
+    return pltpu.VMEM(shape, jnp.float32)
+
+
+def final(*shape):
     return jax.ShapeDtypeStruct(shape, jnp.float32)
 
 
@@ -344,11 +355,8 @@
     fill(high, halo + rows, halo, theirs_halo, halo)
 
     lane2 = lane_iota(depth)
-    sub2 = lax.broadcasted_iota(jnp.int32, (depth, LANES), 0)
     at_y = member * LANES + core * half - halo + lane2
     in_y = jnp.where((at_y >= 0) & (at_y < total_y), COURANT, 0.0)
-    not_top = sub2 < depth - 1
-    not_low = sub2 > 0
 
     def next_y(f):
         return pltpu.roll(f, LANES - 1, 1)
@@ -356,42 +364,58 @@
     def prev_y(f):
         return pltpu.roll(f, 1, 1)
 
+    sub = lax.broadcasted_iota(jnp.int32, (SUBS, LANES), 0)
+
     def next_z(f):
-        return jnp.where(not_top, pltpu.roll(f, depth - 1, 0), 0.0)
+        low, high = pltpu.roll(f[:SUBS], SUBS - 1, 0), pltpu.roll(f[SUBS:], SUBS - 1, 0)
+        return jnp.concatenate(
+            [jnp.where(sub < SUBS - 1, low, high), jnp.where(sub < SUBS - 1, high, 0.0)], axis=0
+        )
 
     def prev_z(f):
-        return jnp.where(not_low, pltpu.roll(f, 1, 0), 0.0)
+        low, high = pltpu.roll(f[:SUBS], 1, 0), pltpu.roll(f[SUBS:], 1, 0)
+        return jnp.concatenate(
+            [jnp.where(sub > 0, low, 0.0), jnp.where(sub > 0, high, low)], axis=0
+        )
 
     first_x = group * rows - halo
 
     def step(n, _):
-        middle = n.astype(jnp.float32) + 0.5
         pulse = pulses(n)
 
-        def row(i, carry):
+        def rows_at(b, carry):
             hy_behind, hz_behind = carry
-            at_x = first_x + i
-            inside = jnp.where((at_x >= 0) & (at_x < total_x), 1.0, 0.0)
-            scale = in_y * inside
-            ex, ey, ez = field[i, 0], field[i, 1], field[i, 2]
-            hx, hy, hz = field[i, 3], field[i, 4], field[i, 5]
-            ey_on, ez_on = field[i + 1, 1], field[i + 1, 2]
-            hx = hx - scale * ((next_y(ez) - ez) - (next_z(ey) - ey))
-            hy = hy - scale * ((next_z(ex) - ex) - (ez_on - ez))
-            hz = hz - scale * ((ey_on - ey) - (next_y(ex) - ex))
-            energy = ex * ex + ey * ey + ez * ez
-            factor = scale / (coef[i, 0] + coef[i, 1] * energy)
-            ex = ex + factor * ((hz - prev_y(hz)) - (hy - prev_z(hy))) + coef[i, 2] * pulse
-            ey = ey + factor * ((hx - prev_z(hx)) - (hz - hz_behind))
-            ez = ez + factor * ((hy - hy_behind) - (hx - prev_y(hx)))
-            field[i, 0], field[i, 1], field[i, 2] = ex, ey, ez
-            field[i, 3], field[i, 4], field[i, 5] = hx, hy, hz
-            hist[0, n, i] = ex[SUBS:]
-            hist[1, n, i] = ey[SUBS:]
-            return hy, hz
+            first = n + b * UNROLL
+            at = [first + u for u in range(UNROLL)]
+            old = [[field[i, a] for a in range(6)] for i in at]
+            ahead = [None, field[first + UNROLL, 1], field[first + UNROLL, 2]]
+            scales = []
+            for u, i in enumerate(at):
+                at_x = first_x + i
+                inside = jnp.where((at_x >= 0) & (at_x < total_x), 1.0, 0.0)
+                scales.append(in_y * inside)
+            for u, i in enumerate(at):
+                ex, ey, ez, hx, hy, hz = old[u]
+                on = old[u + 1] if u + 1 < UNROLL else ahead
+                scale = scales[u]
+                hx = hx - scale * ((next_y(ez) - ez) - (next_z(ey) - ey))
+                hy = hy - scale * ((next_z(ex) - ex) - (on[2] - ez))
+                hz = hz - scale * ((on[1] - ey) - (next_y(ex) - ex))
+                energy = ex * ex + ey * ey + ez * ez
+                factor = scale / (coef[i, 0] + coef[i, 1] * energy)
+                ex = ex + factor * ((hz - prev_y(hz)) - (hy - prev_z(hy))) + coef[i, 2] * pulse
+                ey = ey + factor * ((hx - prev_z(hx)) - (hz - hz_behind))
+                ez = ez + factor * ((hy - hy_behind) - (hx - prev_y(hx)))
+                field[i, 0], field[i, 1], field[i, 2] = ex, ey, ez
+                field[i, 3], field[i, 4], field[i, 5] = hx, hy, hz
+                hist[0, n, i] = ex[SUBS:]
+                hist[1, n, i] = ey[SUBS:]
+                hy_behind, hz_behind = hy, hz
+            return hy_behind, hz_behind
 
         zero = jnp.zeros((depth, LANES), jnp.float32)
-        lax.fori_loop(n, span - 1 - n, row, (zero, zero))
+        count = span - 1 - 2 * n
+        lax.fori_loop(0, (count + UNROLL - 1) // UNROLL, rows_at, (zero, zero))
         return 0
 
     def pulses(n):
@@ -554,6 +578,7 @@
         [f32(width_x, 10, SUBS, LANES)] * GROUP,
         (fields, material, source_mask),
         name="quarters",
+        near=False,
     )
     pieces = [pieces[0]] + [shift_xor(pieces[j], j) for j in range(1, GROUP)]
 
@@ -606,9 +631,9 @@
         (eps_table, kerr_table, own, low, high, theirs, theirs_halo),
         in_specs=[SMEM, SMEM] + [VMEM] * 5,
         scratch=[
-            pltpu.VMEM((span, 6, 2 * SUBS, LANES), jnp.float32),
-            pltpu.VMEM((span, 3, 2 * SUBS, LANES), jnp.float32),
-            pltpu.VMEM((2, STEPS, span, SUBS, LANES), jnp.float32),
+            pltpu.VMEM((span + UNROLL, 6, 2 * SUBS, LANES), jnp.float32),
+            pltpu.VMEM((span + UNROLL, 3, 2 * SUBS, LANES), jnp.float32),
+            pltpu.VMEM((2, STEPS, span + UNROLL, SUBS, LANES), jnp.float32),
         ],
         name="steps",
     )
@@ -625,13 +650,13 @@
     stacked = call(stack_body, f32(GROUP, 4, SUBS, LANES), turned, name="stack")
     image = call(
         column_transform_body,
-        f32(width_x, 8, col_count),
+        final(width_x, 8, col_count),
         (chirp_y, stacked, swap_cores(stacked)),
         name="colt",
     )
     state = call(
         functools.partial(unquarter_body, place),
-        f32(6, width_x, SUBS, span_y),
+        final(6, width_x, SUBS, span_y),
         joined,
         name="unquarter",
     )

time: 202 us -> 101 us (0.50)
  Pallas kernels: 130 us -> 34.9 us
  local copies, waits for them, and re-layouts: 7.39 us -> 0 us
  waiting for transfers between devices: 35.8 us -> 39.1 us
  other arithmetic: 6.83 us -> 4.8 us
    pallas_call x10, Pallas kernels: 130 us -> 34.9 us  [call(): pl.pallas_call(body, out_shape=out_shape, in_specs=in_specs or [VMEM] * l...]
    unnamed x36 -> x0, local copies, waits for them, and re-layouts: 7.39 us -> none
    ppermute x12, waiting for transfers between devices: 19.9 us -> 23.3 us  [shift_xor(): return lax.ppermute(array, 'lat', [(i, i ^ by) for i in range(count)])]
  transfers between devices with their start and end apart: 18 -> 18, of which waited for: 9 -> 10; matrix products, arithmetic and copies ran while one was open for 3% -> 5% of each run, Pallas kernels for 6% -> 5%
where the time goes in v2:
time: 101 us
  waiting for transfers between devices  39.1 us (39%)
  Pallas kernels  34.9 us (35%)
  starting transfers between devices  21.6 us (21%)
  other arithmetic  4.8 us (5%)
    pallas_call x10, Pallas kernels, call(): pl.pallas_call(body, out_shape=out_shape, in_specs=in_specs or [VMEM] * l...  34.9 us
    ppermute x12, waiting for transfers between devices, shift_xor(): return lax.ppermute(array, 'lat', [(i, i ^ by) for i in range(count)])  23.3 us
    ppermute x12, starting transfers between devices, shift_xor(): return lax.ppermute(array, 'lat', [(i, i ^ by) for i in range(count)])  16.1 us
    ppermute x1, waiting for transfers between devices, local_regrouped(): low = lax.ppermute(up, 'lat', upward)  11.6 us
    mul x2, other arithmetic, chirp_parts(): return (jnp.cos(phase) * scale, jnp.sin(phase) * scale)  4.48 us
    ppermute x1, waiting for transfers between devices, local_regrouped(): high = lax.ppermute(down, 'lat', [(b, a) for a, b in upward])  4.15 us
    ppermute x1, starting transfers between devices, local_regrouped(): low = lax.ppermute(up, 'lat', upward)  3.52 us
  transfers between devices with their start and end apart: 18, of which 10 were waited for; matrix products, arithmetic and copies ran while one was open for 5% of the time, Pallas kernels for 5%

profile of v2, /device:TPU:0, one launch (start us, length us, event | category | flops | bytes accessed | tf_op | source)
XLA Modules:
  0.0 101.1 jit_solution(10630172356979093861)
XLA Ops:
  0.6 1.8 %quarters.1 = (f32[6,10,8,128]{3,2,1,0:T(8,128)S(1)}, f32[6,10,8,128]{3,2,1,0:T(8,128)S(1)}, f32[6,10,8,128]{3,2,1,0:T(8,128)S(1)}, f32[6,10,8,128]{3,2,1,0:T(8,128)S(1)}) custom-call(f32[6,6,8,512]{3,2,1,0:T(8,128)} %fields.1, s32[6,8,512]{2,1,0:T(8,128)} %material.1, s32[6,8,512]{2,1,0:T(8,128)} %mask.1), custom_call_target="tpu_custom_call" | custom-call | tf_op jit(solution)/shard_map/quarters/pallas_call | solution.py:204
  2.5 3.0 %collective-permute-start = (f32[6,10,8,128]{3,2,1,0:T(8,128)S(1)}, f32[6,10,8,128]{3,2,1,0:T(8,128)S(1)}, u32[]{:S(2)}, u32[]{:S(2)}) collective-permute-start(f32[6,10,8,128]{3,2,1,0:T(8,128)S(1)} %get-tuple-element.21), channel_id=1, source_target_pairs={{0,1},{1,0},{2,3},{3,2},{4,5},{5,4},{6,7},{7,6},{8,9},{9,8},{10,11... | collective-permute-start | bytes 737288 | tf_op jit(solution)/shard_map/ppermute | solution.py:560
  5.5 1.5 %collective-permute-start.1 = (f32[6,10,8,128]{3,2,1,0:T(8,128)S(1)}, f32[6,10,8,128]{3,2,1,0:T(8,128)S(1)}, u32[]{:S(2)}, u32[]{:S(2)}) collective-permute-start(f32[6,10,8,128]{3,2,1,0:T(8,128)S(1)} %get-tuple-element.22), channel_id=1, source_target_pairs={{0,2},{1,3},{2,0},{3,1},{4,6},{5,7},{6,4},{7,5},{8,10},{9,11},{10,... | collective-permute-start | bytes 737288 | tf_op jit(solution)/shard_map/ppermute | solution.py:560
  7.0 5.3 %collective-permute-done.p1 = f32[6,10,8,128]{3,2,1,0:T(8,128)S(1)} collective-permute-done((f32[6,10,8,128]{3,2,1,0:T(8,128)S(1)}, f32[6,10,8,128]{3,2,1,0:T(8,128)S(1)}, u32[]{:S(2)}, u32[]{:S(2)}) %collective-permute-start) | collective-permute-done | bytes 245792 | tf_op jit(solution)/shard_map/ppermute | solution.py:560
  12.3 5.9 %collective-permute-done.1.p2 = f32[6,10,8,128]{3,2,1,0:T(8,128)S(1)} collective-permute-done((f32[6,10,8,128]{3,2,1,0:T(8,128)S(1)}, f32[6,10,8,128]{3,2,1,0:T(8,128)S(1)}, u32[]{:S(2)}, u32[]{:S(2)}) %collective-permute-start.1) | collective-permute-done | bytes 245792 | tf_op jit(solution)/shard_map/ppermute | solution.py:560
  18.4 3.5 %collective-permute-start.3 = (f32[16,10,8,128]{3,2,1,0:T(8,128)S(1)}, f32[16,10,8,128]{3,2,1,0:T(8,128)S(1)}, u32[]{:S(2)}, u32[]{:S(2)}) collective-permute-start(f32[16,10,8,128]{3,2,1,0:T(8,128)S(1)} %get-tuple-element.25), channel_id=1, source_target_pairs={{0,4},{1,5},{2,6},{3,7},{4,8},{5,9},{6,10},{7,11},{8,12},{9,13},{1... | collective-permute-start | bytes 1966088 | tf_op jit(solution)/shard_map/ppermute | solution.py:610
  21.9 1.3 %collective-permute-start.4 = (f32[16,10,8,128]{3,2,1,0:T(8,128)S(1)}, f32[16,10,8,128]{3,2,1,0:T(8,128)S(1)}, u32[]{:S(2)}, u32[]{:S(2)}) collective-permute-start(f32[16,10,8,128]{3,2,1,0:T(8,128)S(1)} %get-tuple-element.26), channel_id=1, source_target_pairs={{4,0},{5,1},{6,2},{7,3},{8,4},{9,5},{10,6},{11,7},{12,8},{13,9},{1... | collective-permute-start | bytes 1966088 | tf_op jit(solution)/shard_map/ppermute | solution.py:611
  23.2 11.6 %collective-permute-done.3.low = f32[16,10,8,128]{3,2,1,0:T(8,128)S(1)} collective-permute-done((f32[16,10,8,128]{3,2,1,0:T(8,128)S(1)}, f32[16,10,8,128]{3,2,1,0:T(8,128)S(1)}, u32[]{:S(2)}, u32[]{:S(2)}) %collective-permute-start.3) | collective-permute-done | bytes 655392 | tf_op jit(solution)/shard_map/ppermute | solution.py:610
  34.7 4.2 %collective-permute-done.4.high = f32[16,10,8,128]{3,2,1,0:T(8,128)S(1)} collective-permute-done((f32[16,10,8,128]{3,2,1,0:T(8,128)S(1)}, f32[16,10,8,128]{3,2,1,0:T(8,128)S(1)}, u32[]{:S(2)}, u32[]{:S(2)}) %collective-permute-start.4) | collective-permute-done | bytes 655392 | tf_op jit(solution)/shard_map/ppermute | solution.py:611
  38.9 2.7 %win_halo.1 = f32[32,8,8,128]{3,2,1,0:T(8,128)} custom-call(f32[16,10,8,128]{3,2,1,0:T(8,128)S(1)} %collective-permute-done.3.low, f32[16,10,8,128]{3,2,1,0:T(8,128)S(1)} %collective-permute-done.4.high), custom_call_target="tpu_custom_call" | custom-call | tf_op jit(solution)/shard_map/win_halo/pallas_call | solution.py:204
  41.6 2.1 %win.1 = f32[24,8,8,128]{3,2,1,0:T(8,128)S(1)} custom-call(f32[24,10,8,128]{3,2,1,0:T(8,128)S(1)} %get-tuple-element.24.packed.own), custom_call_target="tpu_custom_call" | custom-call | tf_op jit(solution)/shard_map/win/pallas_call | solution.py:204
  43.7 0.6 collective-permute-start.5
  44.5 4.3 %cosine_multiply_fusion.1 = (f32[1,512,256]{2,1,0:T(8,128)S(1)}, f32[1,512,256]{2,1,0:T(8,128)S(1)}, f32[1,512,256]{2,1,0:T(8,128)S(1)}, f32[1,512,256]{2,1,0:T(8,128)S(1)}) fusion(s32[256]{0:T(256)S(1)} %iota_add_fusion, s32[512]{0:T(512)S(1)} %fusion.24), kind=kLoop, calls=%fused_computation.18 | loop fusion | flops 4456448 | bytes 2100224 | tf_op jit(solution)/shard_map/mul | solution.py:500
  48.8 24.8 %steps.1 = (f32[12,6,8,128]{3,2,1,0:T(8,128)S(1)}, f32[12,6,8,128]{3,2,1,0:T(8,128)S(1)}, f32[4,24,128]{2,1,0:T(8,128)S(1)}) custom-call(f32[4]{0:T(128)} %eps.1, f32[4]{0:T(128)} %kerr.1, f32[24,10,8,128]{3,2,1,0:T(8,128)S(1)} %get-tuple-element.24.packed.own, f32[16,10,8,128]{3,2,1,0:T(8,128)S(1)} %collective-permute-done.3.low, ...), custom_call_target="tpu_custom_call" | custom-call | tf_op jit(solution)/shard_map/steps/pallas_call | solution.py:204
  73.6 1.6 %collective-permute-start.11 = (f32[4,24,128]{2,1,0:T(8,128)S(1)}, f32[4,24,128]{2,1,0:T(8,128)S(1)}, u32[]{:S(2)}, u32[]{:S(2)}) collective-permute-start(f32[4,24,128]{2,1,0:T(8,128)S(1)} %get-tuple-element.33.refs_0_), channel_id=1, source_target_pairs={{0,4},{1,5},{2,6},{3,7},{4,0},{5,1},{6,2},{7,3},{8,12},{9,13},{10,... | collective-permute-start | bytes 147464 | tf_op jit(solution)/shard_map/ppermute | solution.py:560
  75.2 1.1 %collective-permute-start.12 = (f32[4,24,128]{2,1,0:T(8,128)S(1)}, f32[4,24,128]{2,1,0:T(8,128)S(1)}, u32[]{:S(2)}, u32[]{:S(2)}) collective-permute-start(f32[4,24,128]{2,1,0:T(8,128)S(1)} %get-tuple-element.33.refs_0_), channel_id=1, source_target_pairs={{0,8},{1,9},{2,10},{3,11},{4,12},{5,13},{6,14},{7,15},{8,0},{9,1},... | collective-permute-start | bytes 147464 | tf_op jit(solution)/shard_map/ppermute | solution.py:560
  76.3 1.8 %collective-permute-start.13 = (f32[4,24,128]{2,1,0:T(8,128)S(1)}, f32[4,24,128]{2,1,0:T(8,128)S(1)}, u32[]{:S(2)}, u32[]{:S(2)}) collective-permute-start(f32[4,24,128]{2,1,0:T(8,128)S(1)} %get-tuple-element.33.refs_0_), channel_id=1, source_target_pairs={{0,12},{1,13},{2,14},{3,15},{4,8},{5,9},{6,10},{7,11},{8,4},{9,5},... | collective-permute-start | bytes 147464 | tf_op jit(solution)/shard_map/ppermute | solution.py:560
  78.1 4.3 %collective-permute-done.12.refs_2_ = f32[4,24,128]{2,1,0:T(8,128)S(1)} collective-permute-done((f32[4,24,128]{2,1,0:T(8,128)S(1)}, f32[4,24,128]{2,1,0:T(8,128)S(1)}, u32[]{:S(2)}, u32[]{:S(2)}) %collective-permute-start.12) | collective-permute-done | bytes 49184 | tf_op jit(solution)/shard_map/ppermute | solution.py:560
  82.4 0.3 rowt.1
  82.7 1.5 %collective-permute-start.14 = (f32[4,8,128]{2,1,0:T(8,128)S(1)}, f32[4,8,128]{2,1,0:T(8,128)S(1)}, u32[]{:S(2)}, u32[]{:S(2)}) collective-permute-start(f32[4,8,128]{2,1,0:T(8,128)S(1)} %get-tuple-element.35), channel_id=1, source_target_pairs={{0,1},{1,0},{2,3},{3,2},{4,5},{5,4},{6,7},{7,6},{8,9},{9,8},{10,11... | collective-permute-start | bytes 49160 | tf_op jit(solution)/shard_map/ppermute | solution.py:560
  84.2 0.6 collective-permute-start.15
  84.8 1.5 %collective-permute-start.16 = (f32[4,8,128]{2,1,0:T(8,128)S(1)}, f32[4,8,128]{2,1,0:T(8,128)S(1)}, u32[]{:S(2)}, u32[]{:S(2)}) collective-permute-start(f32[4,8,128]{2,1,0:T(8,128)S(1)} %get-tuple-element.37), channel_id=1, source_target_pairs={{0,3},{1,2},{2,1},{3,0},{4,7},{5,6},{6,5},{7,4},{8,11},{9,10},{10,... | collective-permute-start | bytes 49160 | tf_op jit(solution)/shard_map/ppermute | solution.py:560
  86.5 1.4 %collective-permute-done.15.p2 = f32[4,8,128]{2,1,0:T(8,128)S(1)} collective-permute-done((f32[4,8,128]{2,1,0:T(8,128)S(1)}, f32[4,8,128]{2,1,0:T(8,128)S(1)}, u32[]{:S(2)}, u32[]{:S(2)}) %collective-permute-start.15) | collective-permute-done | bytes 16416 | tf_op jit(solution)/shard_map/ppermute | solution.py:560
  88.0 1.5 %collective-permute-done.16.p3 = f32[4,8,128]{2,1,0:T(8,128)S(1)} collective-permute-done((f32[4,8,128]{2,1,0:T(8,128)S(1)}, f32[4,8,128]{2,1,0:T(8,128)S(1)}, u32[]{:S(2)}, u32[]{:S(2)}) %collective-permute-start.16) | collective-permute-done | bytes 16416 | tf_op jit(solution)/shard_map/ppermute | solution.py:560
  89.4 0.4 join.1
  89.8 1.6 %collective-permute-start.10 = (f32[6,6,8,128]{3,2,1,0:T(8,128)S(1)}, f32[6,6,8,128]{3,2,1,0:T(8,128)S(1)}, u32[]{:S(2)}, u32[]{:S(2)}) collective-permute-start(f32[6,6,8,128]{3,2,1,0:T(8,128)S(1)} %get-tuple-element.32), channel_id=1, source_target_pairs={{0,3},{1,2},{2,1},{3,0},{4,7},{5,6},{6,5},{7,4},{8,11},{9,10},{10,... | collective-permute-start | bytes 442376 | tf_op jit(solution)/shard_map/ppermute | solution.py:560
  91.4 1.4 %collective-permute-start.8 = (f32[6,6,8,128]{3,2,1,0:T(8,128)S(1)}, f32[6,6,8,128]{3,2,1,0:T(8,128)S(1)}, u32[]{:S(2)}, u32[]{:S(2)}) collective-permute-start(f32[6,6,8,128]{3,2,1,0:T(8,128)S(1)} %get-tuple-element.30), channel_id=1, source_target_pairs={{0,1},{1,0},{2,3},{3,2},{4,5},{5,4},{6,7},{7,6},{8,9},{9,8},{10,11... | collective-permute-start | bytes 442376 | tf_op jit(solution)/shard_map/ppermute | solution.py:560
  92.8 0.6 collective-permute-start.9
  93.5 1.8 %colt.1 = f32[6,8,256]{2,1,0:T(8,128)} custom-call(f32[2,2,512,256]{3,2,1,0:T(8,128)S(1)} %pad_maximum_fusion.chirp_y, f32[4,4,8,128]{3,2,1,0:T(8,128)S(1)} %stack.49.mine, f32[4,4,8,128]{3,2,1,0:T(8,128)S(1)} %collective-permute-done.17.theirs), custom_call_target="tpu_custom_call" | custom-call | tf_op jit(solution)/shard_map/colt/pallas_call | solution.py:204
  95.4 2.2 %collective-permute-done.10.p3 = f32[6,6,8,128]{3,2,1,0:T(8,128)S(1)} collective-permute-done((f32[6,6,8,128]{3,2,1,0:T(8,128)S(1)}, f32[6,6,8,128]{3,2,1,0:T(8,128)S(1)}, u32[]{:S(2)}, u32[]{:S(2)}) %collective-permute-start.10) | collective-permute-done | bytes 147488 | tf_op jit(solution)/shard_map/ppermute | solution.py:560
  97.5 2.7 %collective-permute-done.8.p1 = f32[6,6,8,128]{3,2,1,0:T(8,128)S(1)} collective-permute-done((f32[6,6,8,128]{3,2,1,0:T(8,128)S(1)}, f32[6,6,8,128]{3,2,1,0:T(8,128)S(1)}, u32[]{:S(2)}, u32[]{:S(2)}) %collective-permute-start.8) | collective-permute-done | bytes 147488 | tf_op jit(solution)/shard_map/ppermute | solution.py:560
  100.2 0.9 unquarter.1
  (24 shorter events, 0.9 us)
Async XLA Ops:
  2.5 9.8 %collective-permute-start = (f32[6,10,8,128]{3,2,1,0:T(8,128)S(1)}, f32[6,10,8,128]{3,2,1,0:T(8,128)S(1)}, u32[]{:S(2)}, u32[]{:S(2)}) collective-permute-start(f32[6,10,8,128]{3,2,1,0:T(8,128)S(1)} %get-tuple-element.21), channel_id=1, source_target_pairs={{0,1},{1,0},{2,3},{3,2},{4,5},{5,4},{6,7},{7,6},{8,9},{9,8},{10,11... | collective-permute-start | bytes 737288 | tf_op jit(solution)/shard_map/ppermute | solution.py:560
  5.5 12.7 %collective-permute-start.1 = (f32[6,10,8,128]{3,2,1,0:T(8,128)S(1)}, f32[6,10,8,128]{3,2,1,0:T(8,128)S(1)}, u32[]{:S(2)}, u32[]{:S(2)}) collective-permute-start(f32[6,10,8,128]{3,2,1,0:T(8,128)S(1)} %get-tuple-element.22), channel_id=1, source_target_pairs={{0,2},{1,3},{2,0},{3,1},{4,6},{5,7},{6,4},{7,5},{8,10},{9,11},{10,... | collective-permute-start | bytes 737288 | tf_op jit(solution)/shard_map/ppermute | solution.py:560
  7.0 11.2 %collective-permute-start.2 = (f32[6,10,8,128]{3,2,1,0:T(8,128)S(1)}, f32[6,10,8,128]{3,2,1,0:T(8,128)S(1)}, u32[]{:S(2)}, u32[]{:S(2)}) collective-permute-start(f32[6,10,8,128]{3,2,1,0:T(8,128)S(1)} %get-tuple-element.23), channel_id=1, source_target_pairs={{0,3},{1,2},{2,1},{3,0},{4,7},{5,6},{6,5},{7,4},{8,11},{9,10},{10,... | collective-permute-start | bytes 737288 | tf_op jit(solution)/shard_map/ppermute | solution.py:560
  18.4 16.4 %collective-permute-start.3 = (f32[16,10,8,128]{3,2,1,0:T(8,128)S(1)}, f32[16,10,8,128]{3,2,1,0:T(8,128)S(1)}, u32[]{:S(2)}, u32[]{:S(2)}) collective-permute-start(f32[16,10,8,128]{3,2,1,0:T(8,128)S(1)} %get-tuple-element.25), channel_id=1, source_target_pairs={{0,4},{1,5},{2,6},{3,7},{4,8},{5,9},{6,10},{7,11},{8,12},{9,13},{1... | collective-permute-start | bytes 1966088 | tf_op jit(solution)/shard_map/ppermute | solution.py:610
  21.9 17.0 %collective-permute-start.4 = (f32[16,10,8,128]{3,2,1,0:T(8,128)S(1)}, f32[16,10,8,128]{3,2,1,0:T(8,128)S(1)}, u32[]{:S(2)}, u32[]{:S(2)}) collective-permute-start(f32[16,10,8,128]{3,2,1,0:T(8,128)S(1)} %get-tuple-element.26), channel_id=1, source_target_pairs={{4,0},{5,1},{6,2},{7,3},{8,4},{9,5},{10,6},{11,7},{12,8},{13,9},{1... | collective-permute-start | bytes 1966088 | tf_op jit(solution)/shard_map/ppermute | solution.py:611
  41.6 7.2 %collective-permute-start.6 = (f32[32,8,8,128]{3,2,1,0:T(8,128)}, f32[32,8,8,128]{3,2,1,0:T(8,128)S(1)}, u32[]{:S(2)}, u32[]{:S(2)}) collective-permute-start(f32[32,8,8,128]{3,2,1,0:T(8,128)} %win_halo.1), channel_id=1, source_target_pairs={{0,16},{16,0},{1,17},{17,1},{2,18},{18,2},{3,19},{19,3},{4,20},{20... | collective-permute-start | bytes 3145736 | tf_op jit(solution)/shard_map/ppermute | solution.py:564
  43.7 5.1 %collective-permute-start.5 = (f32[24,8,8,128]{3,2,1,0:T(8,128)S(1)}, f32[24,8,8,128]{3,2,1,0:T(8,128)S(1)}, u32[]{:S(2)}, u32[]{:S(2)}) collective-permute-start(f32[24,8,8,128]{3,2,1,0:T(8,128)S(1)} %win.1), channel_id=1, source_target_pairs={{0,16},{16,0},{1,17},{17,1},{2,18},{18,2},{3,19},{19,3},{4,20},{20... | collective-permute-start | bytes 2359304 | tf_op jit(solution)/shard_map/ppermute | solution.py:564
  73.6 15.9 %collective-permute-start.7 = (f32[12,6,8,128]{3,2,1,0:T(8,128)S(1)}, f32[12,6,8,128]{3,2,1,0:T(8,128)S(1)}, u32[]{:S(2)}, u32[]{:S(2)}) collective-permute-start(f32[12,6,8,128]{3,2,1,0:T(8,128)S(1)} %get-tuple-element.28), channel_id=1, source_target_pairs={{0,16},{16,0},{1,17},{17,1},{2,18},{18,2},{3,19},{19,3},{4,20},{20... | collective-permute-start | bytes 884744 | tf_op jit(solution)/shard_map/ppermute | solution.py:564
  73.6 4.5 %collective-permute-start.11 = (f32[4,24,128]{2,1,0:T(8,128)S(1)}, f32[4,24,128]{2,1,0:T(8,128)S(1)}, u32[]{:S(2)}, u32[]{:S(2)}) collective-permute-start(f32[4,24,128]{2,1,0:T(8,128)S(1)} %get-tuple-element.33.refs_0_), channel_id=1, source_target_pairs={{0,4},{1,5},{2,6},{3,7},{4,0},{5,1},{6,2},{7,3},{8,12},{9,13},{10,... | collective-permute-start | bytes 147464 | tf_op jit(solution)/shard_map/ppermute | solution.py:560
  75.2 7.2 %collective-permute-start.12 = (f32[4,24,128]{2,1,0:T(8,128)S(1)}, f32[4,24,128]{2,1,0:T(8,128)S(1)}, u32[]{:S(2)}, u32[]{:S(2)}) collective-permute-start(f32[4,24,128]{2,1,0:T(8,128)S(1)} %get-tuple-element.33.refs_0_), channel_id=1, source_target_pairs={{0,8},{1,9},{2,10},{3,11},{4,12},{5,13},{6,14},{7,15},{8,0},{9,1},... | collective-permute-start | bytes 147464 | tf_op jit(solution)/shard_map/ppermute | solution.py:560
  76.3 6.1 %collective-permute-start.13 = (f32[4,24,128]{2,1,0:T(8,128)S(1)}, f32[4,24,128]{2,1,0:T(8,128)S(1)}, u32[]{:S(2)}, u32[]{:S(2)}) collective-permute-start(f32[4,24,128]{2,1,0:T(8,128)S(1)} %get-tuple-element.33.refs_0_), channel_id=1, source_target_pairs={{0,12},{1,13},{2,14},{3,15},{4,8},{5,9},{6,10},{7,11},{8,4},{9,5},... | collective-permute-start | bytes 147464 | tf_op jit(solution)/shard_map/ppermute | solution.py:560
  82.7 3.8 %collective-permute-start.14 = (f32[4,8,128]{2,1,0:T(8,128)S(1)}, f32[4,8,128]{2,1,0:T(8,128)S(1)}, u32[]{:S(2)}, u32[]{:S(2)}) collective-permute-start(f32[4,8,128]{2,1,0:T(8,128)S(1)} %get-tuple-element.35), channel_id=1, source_target_pairs={{0,1},{1,0},{2,3},{3,2},{4,5},{5,4},{6,7},{7,6},{8,9},{9,8},{10,11... | collective-permute-start | bytes 49160 | tf_op jit(solution)/shard_map/ppermute | solution.py:560
  84.2 3.7 %collective-permute-start.15 = (f32[4,8,128]{2,1,0:T(8,128)S(1)}, f32[4,8,128]{2,1,0:T(8,128)S(1)}, u32[]{:S(2)}, u32[]{:S(2)}) collective-permute-start(f32[4,8,128]{2,1,0:T(8,128)S(1)} %get-tuple-element.36), channel_id=1, source_target_pairs={{0,2},{1,3},{2,0},{3,1},{4,6},{5,7},{6,4},{7,5},{8,10},{9,11},{10,... | collective-permute-start | bytes 49160 | tf_op jit(solution)/shard_map/ppermute | solution.py:560
  84.8 4.6 %collective-permute-start.16 = (f32[4,8,128]{2,1,0:T(8,128)S(1)}, f32[4,8,128]{2,1,0:T(8,128)S(1)}, u32[]{:S(2)}, u32[]{:S(2)}) collective-permute-start(f32[4,8,128]{2,1,0:T(8,128)S(1)} %get-tuple-element.37), channel_id=1, source_target_pairs={{0,3},{1,2},{2,1},{3,0},{4,7},{5,6},{6,5},{7,4},{8,11},{9,10},{10,... | collective-permute-start | bytes 49160 | tf_op jit(solution)/shard_map/ppermute | solution.py:560
  89.4 4.1 %collective-permute-start.17 = (f32[4,4,8,128]{3,2,1,0:T(8,128)S(1)}, f32[4,4,8,128]{3,2,1,0:T(8,128)S(1)}, u32[]{:S(2)}, u32[]{:S(2)}) collective-permute-start(f32[4,4,8,128]{3,2,1,0:T(8,128)S(1)} %stack.49.mine), channel_id=1, source_target_pairs={{0,16},{16,0},{1,17},{17,1},{2,18},{18,2},{3,19},{19,3},{4,20},{20... | collective-permute-start | bytes 196616 | tf_op jit(solution)/shard_map/ppermute | solution.py:564
  89.8 7.7 %collective-permute-start.10 = (f32[6,6,8,128]{3,2,1,0:T(8,128)S(1)}, f32[6,6,8,128]{3,2,1,0:T(8,128)S(1)}, u32[]{:S(2)}, u32[]{:S(2)}) collective-permute-start(f32[6,6,8,128]{3,2,1,0:T(8,128)S(1)} %get-tuple-element.32), channel_id=1, source_target_pairs={{0,3},{1,2},{2,1},{3,0},{4,7},{5,6},{6,5},{7,4},{8,11},{9,10},{10,... | collective-permute-start | bytes 442376 | tf_op jit(solution)/shard_map/ppermute | solution.py:560
  91.4 8.9 %collective-permute-start.8 = (f32[6,6,8,128]{3,2,1,0:T(8,128)S(1)}, f32[6,6,8,128]{3,2,1,0:T(8,128)S(1)}, u32[]{:S(2)}, u32[]{:S(2)}) collective-permute-start(f32[6,6,8,128]{3,2,1,0:T(8,128)S(1)} %get-tuple-element.30), channel_id=1, source_target_pairs={{0,1},{1,0},{2,3},{3,2},{4,5},{5,4},{6,7},{7,6},{8,9},{9,8},{10,11... | collective-permute-start | bytes 442376 | tf_op jit(solution)/shard_map/ppermute | solution.py:560
  92.8 7.4 %collective-permute-start.9 = (f32[6,6,8,128]{3,2,1,0:T(8,128)S(1)}, f32[6,6,8,128]{3,2,1,0:T(8,128)S(1)}, u32[]{:S(2)}, u32[]{:S(2)}) collective-permute-start(f32[6,6,8,128]{3,2,1,0:T(8,128)S(1)} %get-tuple-element.31), channel_id=1, source_target_pairs={{0,2},{1,3},{2,0},{3,1},{4,6},{5,7},{6,4},{7,5},{8,10},{9,11},{10,... | collective-permute-start | bytes 442376 | tf_op jit(solution)/shard_map/ppermute | solution.py:560
